TPU v7x, 256 devices: a whole 4x4x8 slice. The times are simulated.
256 devices in a mesh: tm: 32 (over z_lo, x, core), cells: 8 (over y, z_hi).
Axes of the slice: x: 4, y: 4, z: 8 (z_hi: 2, z_lo: 4; z = z_hi * 4 + z_lo), core: 2. Of those that a mesh axis runs over, the one named last changes fastest.
Arguments:
- hist_bin: int32 [16384, 8192], P('tm', 'cells'), may hold values from 0 to 255
- obs_bin: int32 [16384, 8192], P('tm', 'cells'), may hold values from 0 to 255
- fut_bin: int32 [16384, 8192], P('tm', 'cells'), may hold values from 0 to 255
- region_id: int32 [8192], P('cells'), may hold values from 0 to 127, as said below
- bin_width: float32 [8192], P('cells'), may hold values from 0.005 to 0.05
- bin_offset: float32 [8192], P('cells'), may hold values from -4 to 4
Outputs:
- adjusted: float32 [16384, 8192], P('tm', 'cells')
Inputs may be any that keep to these rules, and one draw needn't show every extreme that they name: `region_id`: every zone of 0 to 127 holds exactly 64 cells.
All inputs are finite; a program needn't handle non-finite values.
Results may differ from a plain program's by a relative error of at most 0.0003.
Values sent between devices are 32-bit elements; how exact they have to be, the bound alone decides.
A program may use at most 64 MiB of HBM per device.

v0:
```python
import math

import jax
import jax.numpy as jnp
from jax import lax
from jax.sharding import PartitionSpec as P

BINS = 256
REGIONS = 128


pool_weight = 0.5


def in_order(blocks, dim):
    blocks = jnp.moveaxis(blocks, 0, dim)
    dims = blocks.shape
    return blocks.reshape(*dims[:dim], dims[dim] * dims[dim + 1], *dims[dim + 2 :])


def copy_for_each(array, axis):
    count = lax.axis_size(axis)
    return lax.all_to_all(
        jnp.broadcast_to(array[None], (count, *array.shape)), axis, 0, 0, tiled=True
    )


def collect(array, axis, dim):
    return in_order(copy_for_each(array, axis), dim)


def tally_bins(stacked, levels):
    series, day_count, cell_count = stacked.shape
    day_block = math.gcd(day_count, max(1, 16384 // cell_count))

    def add_block(turn_index, totals):
        portion = lax.dynamic_slice_in_dim(stacked, turn_index * day_block, day_block, 1)
        matches = (portion[..., None] == levels).astype(jnp.bfloat16)
        return totals + jnp.sum(matches, axis=1, dtype=jnp.float32)

    initial = jnp.zeros((series, cell_count, levels.shape[0]), jnp.float32)
    return lax.fori_loop(0, day_count // day_block, add_block, initial)


def quantile_at(rank_rows, before_rows, pooled_rows):
    ramp_terms = jnp.minimum(
        jnp.maximum(rank_rows[:, :, None] - before_rows[:, None, :], 0.0), pooled_rows[:, None, :]
    )
    return jnp.sum(ramp_terms / jnp.maximum(pooled_rows, 1.0)[:, None, :], axis=2)


def build_table(totals, zone_rows, zone_share, widths, offsets, day_total):
    zone_terms = jnp.einsum(
        "cr,srb->scb",
        zone_rows,
        zone_share,
        precision=lax.Precision.HIGHEST,
        preferred_element_type=jnp.float32,
    )
    pooled = totals + pool_weight * day_total * zone_terms
    bins_total = pooled.shape[2]
    ladder = jnp.arange(bins_total, dtype=jnp.int32)
    upper_mask = (ladder[:, None] <= ladder[None, :]).astype(jnp.float32)
    running = jnp.einsum(
        "scb,bd->scd",
        pooled,
        upper_mask,
        precision=lax.Precision.HIGHEST,
        preferred_element_type=jnp.float32,
    )
    before = running - pooled
    future_rank = before[2] + 0.5 * pooled[2]
    row_count = pooled.shape[1]
    group_size = math.gcd(row_count, 128)
    group_count = row_count // group_size

    def per_group(group_rows):
        rank_rows, obs_before, obs_pooled, hist_before, hist_pooled = group_rows
        return (
            quantile_at(rank_rows, obs_before, obs_pooled),
            quantile_at(rank_rows, hist_before, hist_pooled),
        )

    shaped = (
        future_rank.reshape(group_count, group_size, bins_total),
        before[1].reshape(group_count, group_size, bins_total),
        pooled[1].reshape(group_count, group_size, bins_total),
        before[0].reshape(group_count, group_size, bins_total),
        pooled[0].reshape(group_count, group_size, bins_total),
    )
    quant_obs, quant_hist = lax.map(per_group, shaped)
    quant_obs = quant_obs.reshape(row_count, bins_total)
    quant_hist = quant_hist.reshape(row_count, bins_total)
    centers = (ladder.astype(jnp.float32) + 0.5)[None, :]
    return offsets[:, None] + widths[:, None] * (centers + quant_obs - quant_hist)


def apply_table(fut_bin, lookup, levels):
    day_count, cell_count = fut_bin.shape
    day_block = math.gcd(day_count, max(1, 16384 // cell_count))
    folded = fut_bin.reshape(day_count // day_block, day_block, cell_count)

    def select_rows(bins_rows):
        matches = bins_rows[..., None] == levels
        return jnp.sum(jnp.where(matches, lookup[None], 0.0), axis=2)

    return lax.map(select_rows, folded).reshape(day_count, cell_count)


def body(hist_bin, obs_bin, fut_bin, region_id, bin_width, bin_offset):
    day_count, cell_count = hist_bin.shape
    levels = jnp.arange(BINS, dtype=jnp.int32)
    stacked = jnp.stack([hist_bin, obs_bin, fut_bin])
    totals = tally_bins(stacked, levels)
    zone_rows = (region_id[:, None] == jnp.arange(REGIONS, dtype=jnp.int32)[None, :]).astype(
        jnp.float32
    )
    zone_part = jnp.einsum(
        "cr,scb->srb",
        zone_rows,
        totals,
        precision=lax.Precision.HIGHEST,
        preferred_element_type=jnp.float32,
    )
    zone_counts = lax.psum(zone_part, ("tm", "cells"))
    zone_share = zone_counts / jnp.sum(zone_counts, axis=2, keepdims=True)
    day_total = day_count * lax.axis_size("tm")
    share_rows = lax.psum_scatter(totals, "tm", scatter_dimension=1, tiled=True)
    share_count = share_rows.shape[1]
    first_row = lax.axis_index("tm") * share_count
    share_zones = lax.dynamic_slice_in_dim(zone_rows, first_row, share_count, 0)
    share_widths = lax.dynamic_slice_in_dim(bin_width, first_row, share_count, 0)
    share_offsets = lax.dynamic_slice_in_dim(bin_offset, first_row, share_count, 0)
    partial_table = build_table(
        share_rows, share_zones, zone_share, share_widths, share_offsets, day_total
    )
    lookup = collect(partial_table, "tm", 0)
    return apply_table(fut_bin, lookup, levels)


def solution(mesh):
    placed = (
        P("tm", "cells"),
        P("tm", "cells"),
        P("tm", "cells"),
        P("cells"),
        P("cells"),
        P("cells"),
    )
    return jax.shard_map(
        body, mesh=mesh, in_specs=placed, out_specs=P("tm", "cells"), check_vma=False
    )
```

profile of v0, /device:TPU:1, one launch (start us, length us, event | category | flops | bytes accessed | tf_op | source)
XLA Modules:
  0.0 995.9 jit_solution(16803068548199994457)
XLA Ops:
  7.4 6.6 pad_add_fusion
  14.0 453.7 %while.31 = (s32[]{:T(128)}, f32[3,1024,256]{2,1,0:T(8,128)}, s32[3,512,1024]{2,1,0:T(8,128)}, s32[]{:T(128)}, s32[]{:T(128)}, /*index=5*/s32[]{:T(128)}, s32[]{:T(128)}) while((s32[]{:T(128)}, f32[3,1024,256]{2,1,0:T(8,128)}, s32[3,512,1024]{2,1,0:T(8,128)}, s32[]{:T(128)}, s32[]{:T(128)}, /*index=5*/s32[]{:T(128)}, ...), condition=%wide.region_2.0_spmd.clone, body=%wide.region_0.0_spmd.clone.sunk | while | flops 51118084 | bytes 13172873 | solution.py:42
  15.0 9.3 convert_reduce_fusion.2
  27.3 9.3 convert_reduce_fusion.2
  41.6 9.3 convert_reduce_fusion.2
  55.8 9.3 convert_reduce_fusion.2
  70.0 9.3 convert_reduce_fusion.2
  84.3 9.3 convert_reduce_fusion.2
  98.5 9.3 convert_reduce_fusion.2
  112.7 9.3 convert_reduce_fusion.2
  127.0 9.3 convert_reduce_fusion.2
  141.2 9.3 convert_reduce_fusion.2
  155.5 9.3 convert_reduce_fusion.2
  169.7 9.3 convert_reduce_fusion.2
  183.9 9.3 convert_reduce_fusion.2
  198.2 9.3 convert_reduce_fusion.2
  212.4 9.3 convert_reduce_fusion.2
  226.6 9.3 convert_reduce_fusion.2
  240.9 9.3 convert_reduce_fusion.2
  255.1 9.3 convert_reduce_fusion.2
  269.4 9.3 convert_reduce_fusion.2
  283.6 9.3 convert_reduce_fusion.2
  297.8 9.3 convert_reduce_fusion.2
  312.1 9.3 convert_reduce_fusion.2
  326.3 9.3 convert_reduce_fusion.2
  340.5 9.3 convert_reduce_fusion.2
  354.8 9.3 convert_reduce_fusion.2
  369.0 9.3 convert_reduce_fusion.2
  383.2 9.3 convert_reduce_fusion.2
  397.5 9.3 convert_reduce_fusion.2
  411.7 9.3 convert_reduce_fusion.2
  426.0 9.3 convert_reduce_fusion.2
  440.2 9.3 convert_reduce_fusion.2
  454.4 9.3 convert_reduce_fusion.2
  467.7 5.4 convolution_bitcast_fusion
  475.5 253.2 %all-reduce.2.cloned.1.call-done = f32[3,128,256]{1,2,0:T(8,128)} async-done(((f32[3,128,256]{1,2,0:T(8,128)}), f32[3,128,256]{1,2,0:T(8,128)}) %all-reduce.2.cloned.1.call-update) | async-done | bytes 393232 | tf_op jit(solution)/shard_map/psum | solution.py:125
  736.6 6.3 all-to-all-start
  742.8 26.6 %all-to-all-done = f32[32,32,256]{2,1,0:T(8,128)S(1)} async-done(((f32[32,32,256]{2,1,0:T(8,128)}), f32[32,32,256]{2,1,0:T(8,128)S(1)}, u32[]{:S(2)}, u32[]{:S(2)}) %all-to-all-start) | async-done | bytes 1048608 | tf_op jit(solution)/shard_map/all_to_all | solution.py:23
  769.5 219.0 %while.30 = (s32[]{:T(128)}, f32[32,16,1024]{2,1,0:T(8,128)}, s32[32,16,1024]{2,1,0:T(8,128)}, f32[32,32,256]{2,1,0:T(8,128)S(1)}, s32[]{:T(128)}) while((s32[]{:T(128)}, f32[32,16,1024]{2,1,0:T(8,128)}, s32[32,16,1024]{2,1,0:T(8,128)}, f32[32,32,256]{2,1,0:T(8,128)S(1)}, s32[]{:T(128)}) %tuple.66), condition=%wide.region_10.11_spmd.clone, body=%wide.region_8.10_spmd.clone.sunk | while | flops 12566530 | bytes 1442369 | solution.py:107
  770.3 5.3 select_reduce_fusion.2
  777.2 5.3 select_reduce_fusion.2
  784.0 5.3 select_reduce_fusion.2
  790.8 5.3 select_reduce_fusion.2
  797.7 5.3 select_reduce_fusion.2
  804.5 5.3 select_reduce_fusion.2
  811.4 5.3 select_reduce_fusion.2
  818.2 5.3 select_reduce_fusion.2
  825.1 5.3 select_reduce_fusion.2
  831.9 5.3 select_reduce_fusion.2
  838.8 5.3 select_reduce_fusion.2
  845.6 5.3 select_reduce_fusion.2
  852.4 5.3 select_reduce_fusion.2
  859.3 5.3 select_reduce_fusion.2
  866.1 5.3 select_reduce_fusion.2
  873.0 5.3 select_reduce_fusion.2
  879.8 5.3 select_reduce_fusion.2
  886.7 5.3 select_reduce_fusion.2
  893.5 5.3 select_reduce_fusion.2
  900.3 5.3 select_reduce_fusion.2
  907.2 5.3 select_reduce_fusion.2
  914.0 5.3 select_reduce_fusion.2
  920.9 5.3 select_reduce_fusion.2
  927.7 5.3 select_reduce_fusion.2
  934.6 5.3 select_reduce_fusion.2
  (156 shorter events, 251.4 us)
Async XLA Ops:
  7.4 721.3 %all-reduce.2.cloned.1.call-start = ((), (), s32[]{:S(2)}) async-start(), calls=%async_computation.3 | async-start | bytes 786432 | tf_op jit(solution)/shard_map/psum | solution.py:125
  14.0 453.7 %copy-start = (s32[1024]{0:T(1024)S(1)}, s32[1024]{0:T(1024)}, u32[]{:S(2)}) copy-start(s32[1024]{0:T(1024)} %param.13) | copy-start | bytes 12292
  473.2 256.6 %reduce-scatter.2.cloned.1.call-start = ((), (), s32[]{:S(2)}) async-start(), calls=%async_computation.2 | async-start | bytes 3244032 | tf_op jit(solution)/shard_map/reduce_scatter | solution.py:128
  736.6 32.9 %all-to-all-start = ((f32[32,32,256]{2,1,0:T(8,128)}), f32[32,32,256]{2,1,0:T(8,128)S(1)}, u32[]{:S(2)}, u32[]{:S(2)}) async-start(f32[32,32,256]{2,1,0:T(8,128)} %broadcast_in_dim.68), calls=%async_computation.1 | async-start | bytes 2097152 | tf_op jit(solution)/shard_map/all_to_all | solution.py:23
Sparse Core Ops, SparseCore 0:
  473.3 255.3 all-reduce.1
Sparse Core Ops, SparseCore 1:
  476.2 149.1 reduce-scatter.1
where the time goes:
time: 1000 us; the launch traced here: 996 us
  other arithmetic  606 us (61%)
  waiting for transfers between devices  280 us (28%)
  local copies, waits for them, and re-layouts  80.2 us (8%)
  between operations  14.9 us (1%)
    reduce_sum x32, other arithmetic, add_block(): return totals + jnp.sum(matches, axis=1, dtype=jnp.float32)  297 us
    psum x1, waiting for transfers between devices, body(): zone_counts = lax.psum(zone_part, ('tm', 'cells'))  253 us
    reduce_sum x32, other arithmetic, select_rows(): return jnp.sum(jnp.where(matches, lookup[None], 0.0), axis=2)  171 us
    add x32, other arithmetic, add_block(): return totals + jnp.sum(matches, axis=1, dtype=jnp.float32)  126 us
    dynamic_slice x32, local copies, waits for them, and re-layouts, add_block(): lax.dynamic_slice_in_dim(stacked, turn_index * day_block, day_block, 1)  30.1 us
    eq x32, local copies, waits for them, and re-layouts, select_rows(): matches = bins_rows[..., None] == levels  27 us
    all_to_all x1, waiting for transfers between devices, copy_for_each(): lax.all_to_all(jnp.broadcast_to(array[None], (count, *array.shape)), axis...  26.6 us
    dynamic_update_slice x32, local copies, waits for them, and re-layouts, apply_table(): return lax.map(select_rows, folded).reshape(day_count, cell_count)  20.5 us
  transfers between devices with their start and end apart: 3, of which 2 were waited for; matrix products, arithmetic and copies ran while one was open for 0% of the time, Pallas kernels for 0%

commit v1 on v0

v1 whole, which is shorter than its diff:
```python
import functools

import jax
import jax.numpy as jnp
from jax import lax
from jax.experimental import pallas as pl
from jax.experimental.pallas import tpu as pltpu
from jax.sharding import PartitionSpec as P

BINS = 256
REGIONS = 128
F32 = jnp.float32
BF16 = jnp.bfloat16
POOL_WEIGHT = 0.5

NZ, NX, NK = 4, 4, 2
NC = 8
ROWS = 32


def count_block(xt):
    hi = xt >> 4
    lo = (xt & 15).astype(BF16)
    weight = jnp.where(hi >= 8, 1024.0, 1.0).astype(BF16)
    hi = (hi & 7).astype(BF16)
    zero = jnp.zeros((), BF16)
    one = jnp.ones((), BF16)
    row = lax.broadcasted_iota(jnp.int32, (8, 128), 0)
    lane = lax.broadcasted_iota(jnp.int32, (8, 128), 1)
    slot = lane // 8
    low, high = [], []
    for q in range(8):
        rows = slice(16 * q, 16 * q + 16)
        lo_q, hi_q, w_q = lo[rows], hi[rows], weight[rows]
        lhs = jnp.concatenate([jnp.where(hi_q == float(h), w_q, zero) for h in range(8)], 0)
        rhs = jnp.concatenate([jnp.where(lo_q == float(l), one, zero) for l in range(16)], 0)
        out = lax.dot_general(lhs, rhs, (((1,), (1,)), ((), ())), preferred_element_type=F32)
        for half in range(2):
            idx = (lane % 8) * 16 + half * 8 + row
            packed = jnp.zeros((8, 128), F32)
            for h in range(8):
                for m in range(2):
                    at = 16 * h + 8 * half
                    piece = out[at : at + 8, 128 * m : 128 * m + 128]
                    packed = jnp.where(
                        slot == 2 * h + m, jnp.take_along_axis(piece, idx, axis=1), packed
                    )
            upper = jnp.floor(packed * (1.0 / 1024.0))
            low.append(packed - 1024.0 * upper)
            high.append(upper)
    return jnp.concatenate(low, 0), jnp.concatenate(high, 0)


def hist_kernel(h_ref, o_ref, f_ref, r_ref, c_ref, z_ref):
    @pl.when(pl.program_id(0) == 0)
    def _():
        z_ref[...] = jnp.zeros_like(z_ref)

    zone = lax.broadcasted_iota(jnp.int32, (REGIONS, 128), 0)
    pick = (zone == r_ref[...]).astype(BF16)
    for s, x_ref in enumerate((h_ref, o_ref, f_ref)):
        for half, part in enumerate(count_block(x_ref[...].T)):
            c_ref[s, :, 128 * half : 128 * half + 128] = part
            first = jnp.minimum(part, 256.0)
            rest = part - first
            z_ref[half, s] += jnp.dot(
                pick, first.astype(BF16), preferred_element_type=F32
            ) + jnp.dot(pick, rest.astype(BF16), preferred_element_type=F32)


def histogram(hist_bin, obs_bin, fut_bin, region):
    days, cells = hist_bin.shape
    series = pl.BlockSpec((days, 128), lambda j: (0, j))
    return pl.pallas_call(
        hist_kernel,
        grid=(cells // 128,),
        in_specs=[series, series, series, pl.BlockSpec((1, 128), lambda j: (0, j))],
        out_specs=(
            pl.BlockSpec((3, 128, BINS), lambda j: (0, j, 0)),
            pl.BlockSpec((2, 3, REGIONS, 128), lambda j: (0, 0, 0, 0)),
        ),
        out_shape=(
            jax.ShapeDtypeStruct((3, cells, BINS), F32),
            jax.ShapeDtypeStruct((2, 3, REGIONS, 128), F32),
        ),
        name="hist",
    )(hist_bin, obs_bin, fut_bin, region.reshape(1, cells))


def place():
    me = lax.axis_index("tm")
    k = lax.rem(me, NK)
    x = lax.rem(me // NK, NX)
    z = me // (NK * NX)
    return z, x, k


def tm_of(z, x, k):
    return (z * NX + x) * NK + k


def remote(src, dst, send, recv, tm, cells=None):
    target = {"tm": tm} if cells is None else {"tm": tm, "cells": cells}
    return pltpu.make_async_remote_copy(
        src_ref=src,
        dst_ref=dst,
        send_sem=send,
        recv_sem=recv,
        device_id=target,
        device_id_type=pl.DeviceIdType.MESH,
    )


def greet(partners):
    barrier = pltpu.get_barrier_semaphore()
    for target in partners:
        pl.semaphore_signal(
            barrier, inc=1, device_id=target, device_id_type=pl.DeviceIdType.MESH
        )
    pl.semaphore_wait(barrier, len(partners))


def tm_partners(z, x, k):
    near = [{"tm": tm_of(z, x, 1 - k)}]
    near += [{"tm": tm_of(z, lax.rem(x + j, NX), k)} for j in range(1, NX)]
    near += [{"tm": tm_of(lax.rem(z + j, NZ), x, k)} for j in range(1, NZ)]
    return near


def sum_kernel(
    cnt, zin, tot, zone,
    core_in, acc, far_in, side_in, done, last_in,
    z_core, z_acc, z_x, z_acc2, z_z, z_acc3, z_c,
    s_core, r_core, s_far, r_far, s_side, r_side, s_last, r_last,
    zs_core, zr_core, zs_x, zr_x, zs_z, zr_z, zs_c, zr_c, zs_gz, zr_gz, zs_gx, zr_gx, zs_gk, zr_gk,
):
    z, x, k = place()
    c = lax.axis_index("cells")
    other = tm_of(z, x, 1 - k)
    right = lax.rem(x + 1, NX)
    left = lax.rem(x + NX - 1, NX)
    across = lax.rem(x + 2, NX)
    partners = tm_partners(z, x, k)
    partners += [{"cells": lax.rem(c + j, NC)} for j in range(1, NC)]
    greet(partners)

    def run(copies):
        for copy in copies:
            copy.start()
        return copies

    def drain(copies):
        for copy in copies:
            copy.wait_send()

    zc = run([remote(zin.at[1 - k], z_core, zs_core, zr_core, other)])
    order = (across, right, left, x)
    core = run(
        [
            remote(cnt.at[:, :, at, 1 - k], core_in.at[j], s_core.at[j], r_core.at[j], other)
            for j, at in enumerate(order)
        ]
    )
    zc[0].wait_recv()
    z_acc[...] = zin[k] + z_core[...]
    zx = run(
        [
            remote(z_acc.at[:, :, lax.rem(x + j, NX)], z_x.at[j - 1], zs_x.at[j - 1], zr_x.at[j - 1],
                   tm_of(z, lax.rem(x + j, NX), k))
            for j in range(1, NX)
        ]
    )
    core[0].wait_recv()
    acc[0] = cnt[:, :, across, k] + core_in[0]
    far = run(
        [
            remote(acc.at[0, :, 0:2], far_in.at[0], s_far.at[0], r_far.at[0], tm_of(z, right, k)),
            remote(acc.at[0, :, 2:4], far_in.at[1], s_far.at[1], r_far.at[1], tm_of(z, left, k)),
        ]
    )
    core[1].wait_recv()
    acc[1, :, 2:4] = cnt[:, 2:4, right, k] + core_in[1, :, 2:4]
    side = run([remote(acc.at[1, :, 2:4], side_in.at[0, :, 2:4], s_side.at[0], r_side.at[0], tm_of(z, right, k))])
    core[2].wait_recv()
    acc[2, :, 0:2] = cnt[:, 0:2, left, k] + core_in[2, :, 0:2]
    side += run([remote(acc.at[2, :, 0:2], side_in.at[1, :, 0:2], s_side.at[1], r_side.at[1], tm_of(z, left, k))])

    for copy in zx:
        copy.wait_recv()
    z_acc2[...] = z_acc[:, :, x] + z_x[0] + z_x[1] + z_x[2]
    zz = run(
        [
            remote(z_acc2.at[:, lax.rem(z + j, NZ)], z_z.at[j - 1], zs_z.at[j - 1], zr_z.at[j - 1],
                   tm_of(lax.rem(z + j, NZ), x, k))
            for j in range(1, NZ)
        ]
    )

    far[0].wait_recv()
    acc[1, :, 0:2] = cnt[:, 0:2, right, k] + core_in[1, :, 0:2] + far_in[0]
    side += run([remote(acc.at[1, :, 0:2], side_in.at[0, :, 0:2], s_side.at[2], r_side.at[2], tm_of(z, right, k))])
    far[1].wait_recv()
    acc[2, :, 2:4] = cnt[:, 2:4, left, k] + core_in[2, :, 2:4] + far_in[1]
    side += run([remote(acc.at[2, :, 2:4], side_in.at[1, :, 2:4], s_side.at[3], r_side.at[3], tm_of(z, left, k))])

    for copy in zz:
        copy.wait_recv()
    z_acc3[...] = z_acc2[:, z] + z_z[0] + z_z[1] + z_z[2]
    zg = run(
        [
            remote(z_acc3, z_c.at[j - 1], zs_c.at[j - 1], zr_c.at[j - 1], lax.axis_index("tm"),
                   lax.rem(c + j, NC))
            for j in range(1, NC)
        ]
    )

    core[3].wait_recv()
    acc[3] = cnt[:, :, x, k] + core_in[3]
    side[0].wait_recv()
    side[1].wait_recv()
    side[2].wait_recv()
    side[3].wait_recv()
    done[...] = acc[3] + side_in[0] + side_in[1]
    last = run(
        [
            remote(done.at[:, lax.rem(z + j, NZ)], last_in.at[j - 1], s_last.at[j - 1], r_last.at[j - 1],
                   tm_of(lax.rem(z + j, NZ), x, k))
            for j in range(1, NZ)
        ]
    )

    for copy in zg:
        copy.wait_recv()
    total = z_acc3[...] + z_c[0]
    for j in range(1, NC - 1):
        total = total + z_c[j]
    zone[k, x, z] = total
    gz = run(
        [
            remote(zone.at[k, x, z], zone.at[k, x, z], zs_gz.at[j - 1], zr_gz.at[j - 1],
                   tm_of(lax.rem(z + j, NZ), x, k))
            for j in range(1, NZ)
        ]
    )
    for copy in gz:
        copy.wait_recv()
    gx = run(
        [
            remote(zone.at[k, x], zone.at[k, x], zs_gx.at[j - 1], zr_gx.at[j - 1],
                   tm_of(z, lax.rem(x + j, NX), k))
            for j in range(1, NX)
        ]
    )
    for copy in gx:
        copy.wait_recv()
    gk = run([remote(zone.at[k], zone.at[k], zs_gk, zr_gk, other)])

    for copy in last:
        copy.wait_recv()
    tot[...] = done[:, z] + last_in[0] + last_in[1] + last_in[2]
    gk[0].wait_recv()
    for group in (zc, core, zx, far, side, zz, zg, last, gz, gx, gk):
        drain(group)


def sum_days(counts, zones):
    cnt = counts.reshape(3, NZ, NX, NK, ROWS, BINS)
    zin = zones.reshape(2, 3, NZ, NX, 8, 128)
    vmem = pl.BlockSpec(memory_space=pltpu.VMEM)
    dma = pltpu.SemaphoreType.DMA
    block = (3, NZ, ROWS, BINS)
    return pl.pallas_call(
        sum_kernel,
        out_shape=(
            jax.ShapeDtypeStruct((3, ROWS, BINS), F32),
            jax.ShapeDtypeStruct((NK, NX, NZ, 3, 8, 128), F32),
        ),
        in_specs=[vmem, vmem],
        out_specs=(vmem, vmem),
        scratch_shapes=[
            pltpu.VMEM((4, *block), F32),
            pltpu.VMEM((4, *block), F32),
            pltpu.VMEM((2, 3, 2, ROWS, BINS), F32),
            pltpu.VMEM((2, *block), F32),
            pltpu.VMEM(block, F32),
            pltpu.VMEM((3, 3, ROWS, BINS), F32),
            pltpu.VMEM((3, NZ, NX, 8, 128), F32),
            pltpu.VMEM((3, NZ, NX, 8, 128), F32),
            pltpu.VMEM((3, 3, NZ, 8, 128), F32),
            pltpu.VMEM((3, NZ, 8, 128), F32),
            pltpu.VMEM((3, 3, 8, 128), F32),
            pltpu.VMEM((3, 8, 128), F32),
            pltpu.VMEM((7, 3, 8, 128), F32),
            dma((4,)), dma((4,)), dma((2,)), dma((2,)), dma((4,)), dma((4,)), dma((3,)), dma((3,)),
            dma, dma, dma((3,)), dma((3,)), dma((3,)), dma((3,)), dma((7,)), dma((7,)),
            dma((3,)), dma((3,)), dma((3,)), dma((3,)), dma, dma,
        ],
        compiler_params=pltpu.CompilerParams(
            collective_id=0, has_side_effects=True, vmem_limit_bytes=48 * 2**20
        ),
        name="sum_days",
    )(cnt, zin)


def exact_dot(a, b):
    return jnp.dot(a, b, precision=lax.Precision.HIGHEST, preferred_element_type=F32)


def table_kernel(day_total, tot, zone, reg, wid, off, out, bef, poo, rnk, qnt):
    me = lax.axis_index("tm")
    eye = lax.broadcasted_iota(jnp.int32, (ROWS, ROWS), 0) == lax.broadcasted_iota(
        jnp.int32, (ROWS, ROWS), 1
    )

    def column(ref, zero):
        line = jnp.broadcast_to(ref[pl.ds(me, 1), :], (ROWS, ROWS))
        return jnp.sum(jnp.where(eye, line, zero), axis=1, keepdims=True)

    region = column(reg, 0)
    width = column(wid, 0.0)
    offset = column(off, 0.0)
    pick = (lax.broadcasted_iota(jnp.int32, (ROWS, REGIONS), 1) == region).astype(F32)
    upper = (
        lax.broadcasted_iota(jnp.int32, (BINS, BINS), 0)
        <= lax.broadcasted_iota(jnp.int32, (BINS, BINS), 1)
    ).astype(F32)
    for s in range(3):
        halves = []
        for k in range(NK):
            rows = [zone[k, x, z, s] for z in range(NZ) for x in range(NX)]
            halves.append(jnp.concatenate(rows, 0))
        mine = exact_dot(pick, jnp.concatenate(halves, 1))
        share = mine / jnp.sum(mine, axis=1, keepdims=True)
        pooled = tot[s] + POOL_WEIGHT * day_total * share
        before = exact_dot(pooled, upper) - pooled
        if s < 2:
            bef[s] = before
            poo[s] = pooled
        else:
            rnk[...] = before + 0.5 * pooled

    @pl.loop(0, ROWS // 8)
    def _(i):
        at = pl.ds(pl.multiple_of(i * 8, 8), 8)
        rank = rnk[at, :]
        for s in range(2):
            pooled = poo[s, at, :]
            start = bef[s, at, :].T
            cap = pooled.T
            scale = (1.0 / jnp.maximum(pooled, 1.0)).T
            lines = []
            for c in range(8):
                line = rank[c : c + 1, :]
                total = jnp.zeros((8, BINS), F32)
                for b in range(0, BINS, 8):
                    term = line - start[b : b + 8, c : c + 1]
                    term = jnp.minimum(jnp.maximum(term, 0.0), cap[b : b + 8, c : c + 1])
                    total = total + term * scale[b : b + 8, c : c + 1]
                lines.append(jnp.sum(total, axis=0, keepdims=True))
            qnt[s, at, :] = jnp.concatenate(lines, 0)

    centers = lax.broadcasted_iota(jnp.int32, (ROWS, BINS), 1).astype(F32) + 0.5
    out[...] = offset + width * ((centers + qnt[1]) - qnt[0])


def make_table(tot, zone, region, width, offset, day_total):
    return pl.pallas_call(
        functools.partial(table_kernel, float(day_total)),
        out_shape=jax.ShapeDtypeStruct((ROWS, BINS), F32),
        scratch_shapes=[
            pltpu.VMEM((2, ROWS, BINS), F32),
            pltpu.VMEM((2, ROWS, BINS), F32),
            pltpu.VMEM((ROWS, BINS), F32),
            pltpu.VMEM((2, ROWS, BINS), F32),
        ],
        name="table",
    )(tot, zone, region.reshape(-1, ROWS), width.reshape(-1, ROWS), offset.reshape(-1, ROWS))


def gather_kernel(part, out, sz, rz, sx, rx, sf, rf, sk, rk, own):
    z, x, k = place()
    right = lax.rem(x + 1, NX)
    left = lax.rem(x + NX - 1, NX)
    across = lax.rem(x + 2, NX)
    other = tm_of(z, x, 1 - k)
    greet(tm_partners(z, x, k))
    copy = pltpu.make_async_copy(part, out.at[z, x, k], own)
    copy.start()
    zs = [
        remote(part, out.at[z, x, k], sz.at[j - 1], rz.at[j - 1], tm_of(lax.rem(z + j, NZ), x, k))
        for j in range(1, NZ)
    ]
    for one in zs:
        one.start()
    copy.wait()
    for one in zs:
        one.wait_recv()
    xs = [
        remote(out.at[:, x, k], out.at[:, x, k], sx.at[j], rx.at[j], tm_of(z, at, k))
        for j, at in enumerate((right, left))
    ]
    for one in xs:
        one.start()
    ks = [remote(out.at[:, x, k], out.at[:, x, k], sk.at[0], rk.at[0], other)]
    ks[0].start()
    xs[0].wait_recv()
    xs[1].wait_recv()
    source = lax.rem(x + NX - 1 + 2 * k, NX)
    target = lax.rem(x + 1 + 2 * k, NX)
    forward = remote(out.at[:, source, k], out.at[:, source, k], sf, rf, tm_of(z, target, k))
    forward.start()
    for j, at in enumerate((left, right)):
        one = remote(out.at[:, at, k], out.at[:, at, k], sk.at[1 + j], rk.at[1 + j], other)
        one.start()
        ks.append(one)
    forward.wait_recv()
    one = remote(out.at[:, across, k], out.at[:, across, k], sk.at[3], rk.at[3], other)
    one.start()
    ks.append(one)
    for one in ks:
        one.wait_recv()
    for one in zs + xs + [forward] + ks:
        one.wait_send()


def gather_table(part):
    vmem = pl.BlockSpec(memory_space=pltpu.VMEM)
    dma = pltpu.SemaphoreType.DMA
    return pl.pallas_call(
        gather_kernel,
        out_shape=jax.ShapeDtypeStruct((NZ, NX, NK, ROWS, BINS), F32),
        in_specs=[vmem],
        out_specs=vmem,
        scratch_shapes=[
            dma((3,)), dma((3,)), dma((2,)), dma((2,)), dma, dma, dma((4,)), dma((4,)), dma,
        ],
        compiler_params=pltpu.CompilerParams(collective_id=1, has_side_effects=True),
        name="gather_table",
    )(part)


def apply_kernel(x_ref, t_ref, o_ref):
    xt = x_ref[...].T
    low = t_ref[:, 0:128]
    high = t_ref[:, 128:256]
    for at in range(0, xt.shape[1], 128):
        idx = xt[:, at : at + 128]
        inner = idx & 127
        a = jnp.take_along_axis(low, inner, axis=1)
        b = jnp.take_along_axis(high, inner, axis=1)
        o_ref[at : at + 128, :] = jnp.where(idx >= 128, b, a).T


def apply_table(fut_bin, table):
    days, cells = fut_bin.shape
    return pl.pallas_call(
        apply_kernel,
        grid=(cells // 128,),
        in_specs=[
            pl.BlockSpec((days, 128), lambda j: (0, j)),
            pl.BlockSpec((128, BINS), lambda j: (j, 0)),
        ],
        out_specs=pl.BlockSpec((days, 128), lambda j: (0, j)),
        out_shape=jax.ShapeDtypeStruct((days, cells), F32),
        name="apply",
    )(fut_bin, table)


def body(hist_bin, obs_bin, fut_bin, region_id, bin_width, bin_offset):
    days = hist_bin.shape[0] * lax.axis_size("tm")
    counts, zones = histogram(hist_bin, obs_bin, fut_bin, region_id)
    tot, zone = sum_days(counts, zones)
    part = make_table(tot, zone, region_id, bin_width, bin_offset, days)
    table = gather_table(part)
    return apply_table(fut_bin, table.reshape(-1, BINS))


def solution(mesh):
    placed = (
        P("tm", "cells"),
        P("tm", "cells"),
        P("tm", "cells"),
        P("cells"),
        P("cells"),
        P("cells"),
    )
    return jax.shard_map(
        body, mesh=mesh, in_specs=placed, out_specs=P("tm", "cells"), check_vma=False
    )
```

time: 1000 us -> 121 us (0.12)
  other arithmetic: 606 us -> 0 us
  waiting for transfers between devices: 280 us -> 0 us
  Pallas kernels: 0 us -> 114 us
  local copies, waits for them, and re-layouts: 80.2 us -> 6.28 us
  between operations: 14.9 us -> 0.04 us
    reduce_sum x66 -> x0, other arithmetic: 473 us -> none  [the longest x32 297 us: add_block(): return totals + jnp.sum(matches, axis=1, dtype=jnp.float32)]
    psum x1 -> x0, waiting for transfers between devices: 253 us -> none  [body(): zone_counts = lax.psum(zone_part, ('tm', 'cells'))]
    add x34 -> x0, other arithmetic: 126 us -> none  [the longest x32 126 us: add_block(): return totals + jnp.sum(matches, axis=1, dtype=jnp.float32)]
    pallas_call x0 -> x5, Pallas kernels: none -> 114 us  [the longest x1 48.1 us: sum_days(): pl.pallas_call(sum_kernel, out_shape=(jax.ShapeDtypeStruct((3, ROWS, BINS...]
    dynamic_slice x34 -> x0, local copies, waits for them, and re-layouts: 31.6 us -> none  [the longest x32 30.1 us: add_block(): lax.dynamic_slice_in_dim(stacked, turn_index * day_block, day_block, 1)]
    eq x32 -> x0, local copies, waits for them, and re-layouts: 27 us -> none  [select_rows(): matches = bins_rows[..., None] == levels]
    all_to_all x1 -> x0, waiting for transfers between devices: 26.6 us -> none  [copy_for_each(): lax.all_to_all(jnp.broadcast_to(array[None], (count, *array.shape)), axis...]
    dynamic_update_slice x32 -> x0, local copies, waits for them, and re-layouts: 20.5 us -> none  [apply_table(): return lax.map(select_rows, folded).reshape(day_count, cell_count)]
  transfers between devices with their start and end apart: 3 -> 0, of which waited for: 2 -> 0; matrix products, arithmetic and copies ran while one was open for 0% -> 0% of each run, Pallas kernels for 0% -> 0%
where the time goes in v1:
time: 121 us; the launch traced here: 120 us
  Pallas kernels  114 us (94%)
  local copies, waits for them, and re-layouts  6.28 us (5%)
    pallas_call x1, Pallas kernels, sum_days(): pl.pallas_call(sum_kernel, out_shape=(jax.ShapeDtypeStruct((3, ROWS, BINS...  48.1 us
    pallas_call x1, Pallas kernels, histogram(): pl.pallas_call(hist_kernel, grid=(cells // 128,), in_specs=[series, serie...  28.4 us
    pallas_call x1, Pallas kernels, gather_table(): pl.pallas_call(gather_kernel, out_shape=jax.ShapeDtypeStruct((NZ, NX, NK,...  18.3 us
    pallas_call x1, Pallas kernels, make_table(): pl.pallas_call(functools.partial(table_kernel, float(day_total)), out_sha...  11 us
    pallas_call x1, Pallas kernels, apply_table(): pl.pallas_call(apply_kernel, grid=(cells // 128,), in_specs=[pl.BlockSpec...  8.35 us
    unnamed x14, local copies, waits for them, and re-layouts  4.27 us

profile of v1, /device:TPU:1, one launch (start us, length us, event | category | flops | bytes accessed | tf_op | source)
XLA Modules:
  0.0 120.5 jit_solution(5278068163364343546)
XLA Ops:
  0.0 0.0 copy-start.5
  0.0 0.0 copy-start.6
  0.0 28.4 %hist.1 = (f32[3,1024,256]{2,1,0:T(8,128)}, f32[2,3,128,128]{3,2,1,0:T(8,128)}) custom-call(s32[512,1024]{1,0:T(8,128)} %h_ref.1, s32[512,1024]{1,0:T(8,128)} %o_ref.1, s32[512,1024]{1,0:T(8,128)} %x_ref.1, s32[1,1024]{1,0:T(1,128)} %bitcast.7), custom_call_target="tpu_custom_call" | custom-call | tf_op jit(solution)/shard_map/hist/pallas_call | solution.py:74
  28.4 0.0 copy-start.4
  28.4 0.0 copy-start
  28.4 1.9 %copy-done = f32[3,1024,256]{2,1,0:T(8,128)S(1)} copy-done((f32[3,1024,256]{2,1,0:T(8,128)S(1)}, f32[3,1024,256]{2,1,0:T(8,128)}, u32[]{:S(2)}) %copy-start) | copy-done | bytes 3145752
  30.3 0.0 copy-start.1
  30.3 1.0 copy-done.1
  31.3 48.1 %sum_days.1 = (f32[3,32,256]{2,1,0:T(8,128)S(1)}, f32[2,4,4,3,8,128]{5,4,3,2,1,0:T(8,128)S(1)}) custom-call(f32[3,4,4,2,32,256]{5,4,3,2,1,0:T(8,128)S(1)} %bitcast.4, f32[2,3,4,4,8,128]{5,4,3,2,1,0:T(8,128)S(1)} %bitcast.5), custom_call_target="tpu_custom_call" | custom-call | tf_op jit(solution)/shard_map/sum_days/pallas_call | solution.py:272
  79.5 0.0 copy-start.2
  79.5 0.7 copy-done.2
  80.2 0.0 copy-start.3
  80.2 0.6 copy-done.3
  80.8 0.0 copy-done.4
  80.9 0.7 reshape.24.reg
  81.5 0.0 copy-done.5
  81.5 0.7 reshape.25.wid
  82.2 0.0 copy-done.6
  82.2 0.7 reshape.26.off
  82.9 11.0 %table.1.part = f32[32,256]{1,0:T(8,128)} custom-call(f32[3,32,256]{2,1,0:T(8,128)} %copy-done.3, f32[2,4,4,3,8,128]{5,4,3,2,1,0:T(8,128)} %copy-done.2, s32[32,32]{1,0:T(8,128)} %reshape.24.reg, f32[32,32]{1,0:T(8,128)} %reshape.25.wid, f32[32,32]{1,0:T(8,128)} %reshape.26.off), custom_call_target="tpu_custom_call" | custom-call | tf_op jit(solution)/shard_map/table/pallas_call | solution.py:367
  93.8 18.3 %gather_table.1 = f32[4,4,2,32,256]{4,3,2,1,0:T(8,128)} custom-call(f32[32,256]{1,0:T(8,128)} %table.1.part), custom_call_target="tpu_custom_call" | custom-call | tf_op jit(solution)/shard_map/gather_table/pallas_call | solution.py:429
  112.1 8.3 %apply.1 = f32[512,1024]{1,0:T(8,128)} custom-call(s32[512,1024]{1,0:T(8,128)} %x_ref.1, f32[1024,256]{1,0:T(8,128)} %bitcast.6), custom_call_target="tpu_custom_call" | custom-call | tf_op jit(solution)/shard_map/apply/pallas_call | solution.py:456
Async XLA Ops:
  0.0 81.5 %copy-start.5 = (f32[1024]{0:T(1024)S(1)}, f32[1024]{0:T(1024)}, u32[]{:S(2)}) copy-start(f32[1024]{0:T(1024)} %param.10) | copy-start | bytes 12292
  0.0 82.2 %copy-start.6 = (f32[1024]{0:T(1024)S(1)}, f32[1024]{0:T(1024)}, u32[]{:S(2)}) copy-start(f32[1024]{0:T(1024)} %param.11) | copy-start | bytes 12292
  28.4 52.4 %copy-start.4 = (s32[1024]{0:T(1024)S(1)}, s32[1024]{0:T(1024)}, u32[]{:S(2)}) copy-start(s32[1024]{0:T(1024)} %param.9) | copy-start | bytes 12292
  28.4 1.9 %copy-start = (f32[3,1024,256]{2,1,0:T(8,128)S(1)}, f32[3,1024,256]{2,1,0:T(8,128)}, u32[]{:S(2)}) copy-start(f32[3,1024,256]{2,1,0:T(8,128)} %get-tuple-element.9) | copy-start | bytes 9437188
  30.3 1.0 copy-start.1
  79.5 0.7 copy-start.2
  80.2 0.6 copy-start.3

commit v2 on v0

v2 whole, which is shorter than its diff:
```python
import functools

import jax
import jax.numpy as jnp
from jax import lax
from jax.experimental import pallas as pl
from jax.experimental.pallas import tpu as pltpu
from jax.sharding import PartitionSpec as P

BINS = 256
REGIONS = 128
F32 = jnp.float32
BF16 = jnp.bfloat16
POOL_WEIGHT = 0.5

NZ, NX, NK = 4, 4, 2
NC = 8
ROWS = 32


def stage_block(bins, planes, slot):
    xt = bins.T
    hi = xt >> 4
    planes[slot, 0] = (xt & 15).astype(BF16)
    planes[slot, 1] = (hi & 7).astype(BF16)
    planes[slot, 2] = jnp.where(hi >= 8, 1024.0, 1.0).astype(BF16)


def count_block(planes, slot):
    zero = jnp.zeros((), BF16)
    one = jnp.ones((), BF16)
    row = lax.broadcasted_iota(jnp.int32, (8, 128), 0)
    lane = lax.broadcasted_iota(jnp.int32, (8, 128), 1)
    column = lane // 8
    low, high = [], []
    for q in range(8):
        rows = slice(16 * q, 16 * q + 16)
        lo, hi, weight = planes[slot, 0, rows], planes[slot, 1, rows], planes[slot, 2, rows]
        lhs = jnp.concatenate([jnp.where(hi == float(h), weight, zero) for h in range(8)], 0)
        rhs = jnp.concatenate([jnp.where(lo == float(l), one, zero) for l in range(16)], 0)
        out = lax.dot_general(lhs, rhs, (((1,), (1,)), ((), ())), preferred_element_type=F32)
        for half in range(2):
            idx = (lane % 8) * 16 + half * 8 + row
            packed = jnp.zeros((8, 128), F32)
            for h in range(8):
                for m in range(2):
                    at = 16 * h + 8 * half
                    piece = out[at : at + 8, 128 * m : 128 * m + 128]
                    packed = jnp.where(
                        column == 2 * h + m, jnp.take_along_axis(piece, idx, axis=1), packed
                    )
            upper = jnp.floor(packed * (1.0 / 1024.0))
            low.append(packed - 1024.0 * upper)
            high.append(upper)
    return jnp.concatenate(low, 0), jnp.concatenate(high, 0)


def exact_dot(a, b):
    return jnp.dot(a, b, precision=lax.Precision.HIGHEST, preferred_element_type=F32)


def pick_lane(table, idx):
    low, high = table[:, 0:128], table[:, 128:256]
    parts = []
    for at in (0, 128):
        want = idx[:, at : at + 128]
        inner = want & 127
        a = jnp.take_along_axis(low, inner, axis=1)
        b = jnp.take_along_axis(high, inner, axis=1)
        parts.append(jnp.where(want >= 128, b, a))
    return jnp.concatenate(parts, 1)


def make_table(day_total, tot, zone, reg, wid, off, out):
    me = lax.axis_index("tm")
    first = lax.rem(me, 128 // ROWS) * ROWS
    eye = lax.broadcasted_iota(jnp.int32, (ROWS, 128), 1) == first + lax.broadcasted_iota(
        jnp.int32, (ROWS, 128), 0
    )

    def column(ref, zero):
        line = jnp.broadcast_to(ref[pl.ds(me // (128 // ROWS), 1), :], (ROWS, 128))
        return jnp.sum(jnp.where(eye, line, zero), axis=1, keepdims=True)

    region = column(reg, 0)
    width = column(wid, 0.0)
    offset = column(off, 0.0)
    pick = (lax.broadcasted_iota(jnp.int32, (ROWS, REGIONS), 1) == region).astype(F32)
    upper = (
        lax.broadcasted_iota(jnp.int32, (BINS, BINS), 0)
        <= lax.broadcasted_iota(jnp.int32, (BINS, BINS), 1)
    ).astype(F32)
    pooled, stacked = [], []
    for s in range(3):
        halves = []
        for k in range(NK):
            rows = [zone[s, k, x, z] for z in range(NZ) for x in range(NX)]
            halves.append(jnp.concatenate(rows, 0))
        mine = exact_dot(pick, jnp.concatenate(halves, 1))
        share = mine / jnp.sum(mine, axis=1, keepdims=True)
        pooled.append(tot[s] + POOL_WEIGHT * day_total * share)
    filled = [pooled[s] / jnp.maximum(pooled[s], 1.0) for s in range(2)]
    sums = exact_dot(jnp.concatenate(pooled + filled, 0), upper)
    ends = [sums[ROWS * s : ROWS * s + ROWS] for s in range(5)]
    rank = ends[2] - pooled[2] + 0.5 * pooled[2]
    quantile = []
    for s in range(2):
        at = jnp.zeros((ROWS, BINS), jnp.int32)
        for bit in (128, 64, 32, 16, 8, 4, 2, 1):
            full = pick_lane(ends[s], at + (bit - 1)) <= rank
            at = jnp.where(full, at + bit, at)
        at = jnp.minimum(at, BINS - 1)
        before = pick_lane(ends[s] - pooled[s], at)
        size = pick_lane(pooled[s], at)
        inside = jnp.minimum(jnp.maximum(rank - before, 0.0), size) / jnp.maximum(size, 1.0)
        quantile.append(pick_lane(ends[3 + s] - filled[s], at) + inside)
    centers = lax.broadcasted_iota(jnp.int32, (ROWS, BINS), 1).astype(F32) + 0.5
    out[...] = offset + width * ((centers + quantile[1]) - quantile[0])


def place():
    me = lax.axis_index("tm")
    k = lax.rem(me, NK)
    x = lax.rem(me // NK, NX)
    z = me // (NK * NX)
    return z, x, k


def tm_of(z, x, k):
    return (z * NX + x) * NK + k


def remote(src, dst, send, recv, tm, cells=None):
    target = {"tm": tm} if cells is None else {"tm": tm, "cells": cells}
    return pltpu.make_async_remote_copy(
        src_ref=src,
        dst_ref=dst,
        send_sem=send,
        recv_sem=recv,
        device_id=target,
        device_id_type=pl.DeviceIdType.MESH,
    )


def greet(partners):
    barrier = pltpu.get_barrier_semaphore()
    for target in partners:
        pl.semaphore_signal(
            barrier, inc=1, device_id=target, device_id_type=pl.DeviceIdType.MESH
        )
    return lambda: pl.semaphore_wait(barrier, len(partners))


def main_kernel(
    day_total, hist, obs, fut, region, width, offset, table, fut_t,
    xbuf, planes, cnt, zin, core_in, acc, far_in, side_in, done, last_in, tot,
    zone, z_core, z_acc, z_x, z_acc2, z_y, z_acc3, z_z,
    s_in, s_core, r_core, s_far, r_far, s_side, r_side, s_last, r_last,
    zs_core, zr_core, zs_x, zr_x, zs_y, zr_y, zs_z, zr_z, zs_gx, zr_gx, zs_gk, zr_gk,
    gs_z, gr_z, gs_r, gr_r, gs_l, gr_l, gs_f, gr_f, gs_k, gr_k,
):
    z, x, k = place()
    c = lax.axis_index("cells")
    tm = lax.axis_index("tm")
    other = tm_of(z, x, 1 - k)
    right = lax.rem(x + 1, NX)
    left = lax.rem(x + NX - 1, NX)
    across = lax.rem(x + 2, NX)
    to_right, to_left = tm_of(z, right, k), tm_of(z, left, k)
    order = (across, right, left, x)

    series = [
        pltpu.make_async_copy(ref, xbuf.at[s], s_in.at[s])
        for s, ref in enumerate((hist, obs, fut))
    ]
    for copy in series:
        copy.start()
    y, z_hi = c // 2, lax.rem(c, 2)
    z_full = z_hi * NZ + z
    along_y = [lax.rem(y + j, 4) * 2 + z_hi for j in range(1, 4)]
    along_z = []
    for j in range(1, 2 * NZ):
        at = lax.rem(z_full + j, 2 * NZ)
        along_z.append((tm_of(lax.rem(at, NZ), x, k), y * 2 + at // NZ))
    partners = [{"tm": other}]
    partners += [{"tm": tm_of(z, lax.rem(x + j, NX), k)} for j in range(1, NX)]
    partners += [{"cells": at} for at in along_y]
    partners += [{"tm": a, "cells": b} for a, b in along_z]
    met = greet(partners)
    zin[...] = jnp.zeros_like(zin)

    blocks = xbuf.shape[2] // 128
    last_block = 3 * blocks - 1

    def stage(n):
        j = lax.rem(n, blocks)
        at = pl.ds(pl.multiple_of(j * 128, 128), 128)
        stage_block(xbuf[n // blocks, :, at], planes, lax.rem(n, 2))

    def count(first, stop):
        def one(n, carry):
            stage(jnp.minimum(n + 1, last_block))
            s = n // blocks
            j = lax.rem(n, blocks)
            zones = lax.broadcasted_iota(jnp.int32, (REGIONS, 128), 0)
            pick = (zones == region[pl.ds(j, 1), :]).astype(BF16)
            for half, part in enumerate(count_block(planes, lax.rem(n, 2))):
                cnt[s, j // 2, pl.ds(lax.rem(j, 2) * 2, 2), :, :, 128 * half : 128 * half + 128] = (
                    part.reshape(2, NK, ROWS, 128)
                )
                head = jnp.minimum(part, 256.0)
                rest = part - head
                zin[s, half] += jnp.dot(
                    pick, head.astype(BF16), preferred_element_type=F32
                ) + jnp.dot(pick, rest.astype(BF16), preferred_element_type=F32)
            return carry

        lax.fori_loop(first, stop, one, 0)

    started = []

    def run(copies):
        for copy in copies:
            copy.start()
        started.extend(copies)
        return copies

    held = {}

    def p0(s):
        held["zc", s] = run([remote(zin.at[s, 1 - k], z_core.at[s], zs_core.at[s], zr_core.at[s], other)])
        held["core", s] = run(
            [
                remote(cnt.at[s, :, at, 1 - k], core_in.at[s, j], s_core.at[s, j], r_core.at[s, j], other)
                for j, at in enumerate(order)
            ]
        )

    def p1(s):
        core = held["core", s]
        core[0].wait_recv()
        acc[s, 0] = cnt[s, :, across, k] + core_in[s, 0]
        held["far", s] = run(
            [
                remote(acc.at[s, 0, 0:2], far_in.at[s, 0], s_far.at[s, 0], r_far.at[s, 0], to_right),
                remote(acc.at[s, 0, 2:4], far_in.at[s, 1], s_far.at[s, 1], r_far.at[s, 1], to_left),
            ]
        )
        core[1].wait_recv()
        acc[s, 1, 2:4] = cnt[s, 2:4, right, k] + core_in[s, 1, 2:4]
        core[2].wait_recv()
        acc[s, 2, 0:2] = cnt[s, 0:2, left, k] + core_in[s, 2, 0:2]
        held["side", s] = run(
            [
                remote(acc.at[s, 1, 2:4], side_in.at[s, 0, 2:4], s_side.at[s, 0], r_side.at[s, 0], to_right),
                remote(acc.at[s, 2, 0:2], side_in.at[s, 1, 0:2], s_side.at[s, 1], r_side.at[s, 1], to_left),
            ]
        )
        core[3].wait_recv()
        acc[s, 3] = cnt[s, :, x, k] + core_in[s, 3]

    def p2(s):
        far = held["far", s]
        far[0].wait_recv()
        acc[s, 1, 0:2] = cnt[s, 0:2, right, k] + core_in[s, 1, 0:2] + far_in[s, 0]
        far[1].wait_recv()
        acc[s, 2, 2:4] = cnt[s, 2:4, left, k] + core_in[s, 2, 2:4] + far_in[s, 1]
        held["side", s] += run(
            [
                remote(acc.at[s, 1, 0:2], side_in.at[s, 0, 0:2], s_side.at[s, 2], r_side.at[s, 2], to_right),
                remote(acc.at[s, 2, 2:4], side_in.at[s, 1, 2:4], s_side.at[s, 3], r_side.at[s, 3], to_left),
            ]
        )

    def p3(s):
        for copy in held["side", s]:
            copy.wait_recv()
        done[s] = acc[s, 3] + side_in[s, 0] + side_in[s, 1]
        held["last", s] = run(
            [
                remote(done.at[s, lax.rem(z + j, NZ)], last_in.at[s, j - 1], s_last.at[s, j - 1],
                       r_last.at[s, j - 1], tm_of(lax.rem(z + j, NZ), x, k))
                for j in range(1, NZ)
            ]
        )

    def p4(s):
        for copy in held["last", s]:
            copy.wait_recv()
        tot[s] = done[s, z] + last_in[s, 0] + last_in[s, 1] + last_in[s, 2]

    def q1(s):
        held["zc", s][0].wait_recv()
        z_acc[s] = zin[s, k].reshape(NZ, NX, 8, 128) + z_core[s].reshape(NZ, NX, 8, 128)
        held["zx", s] = run(
            [
                remote(z_acc.at[s, :, lax.rem(x + j, NX)], z_x.at[s, j - 1], zs_x.at[s, j - 1],
                       zr_x.at[s, j - 1], tm_of(z, lax.rem(x + j, NX), k))
                for j in range(1, NX)
            ]
        )

    def q2(s):
        for copy in held["zx", s]:
            copy.wait_recv()
        z_acc2[s] = z_acc[s, :, x] + z_x[s, 0] + z_x[s, 1] + z_x[s, 2]
        held["zy", s] = run(
            [
                remote(z_acc2.at[s], z_y.at[s, j], zs_y.at[s, j], zr_y.at[s, j], tm, at)
                for j, at in enumerate(along_y)
            ]
        )

    def q3(s):
        for copy in held["zy", s]:
            copy.wait_recv()
        z_acc3[s] = z_acc2[s] + z_y[s, 0] + z_y[s, 1] + z_y[s, 2]
        held["zz", s] = run(
            [
                remote(z_acc3.at[s], z_z.at[s, j], zs_z.at[s, j], zr_z.at[s, j], *at)
                for j, at in enumerate(along_z)
            ]
        )

    def q4(s):
        for copy in held["zz", s]:
            copy.wait_recv()
        total = z_acc3[s]
        for j in range(2 * NZ - 1):
            total = total + z_z[s, j]
        zone[s, k, x] = total
        held["gx", s] = run(
            [
                remote(zone.at[s, k, x], zone.at[s, k, x], zs_gx.at[s, j - 1], zr_gx.at[s, j - 1],
                       tm_of(z, lax.rem(x + j, NX), k))
                for j in range(1, NX)
            ]
        )

    def q5(s):
        for copy in held["gx", s]:
            copy.wait_recv()
        held["gk", s] = run([remote(zone.at[s, k], zone.at[s, k], zs_gk.at[s], zr_gk.at[s], other)])

    def q6(s):
        held["gk", s][0].wait_recv()

    def turn(first, stop):
        for j in range(first, stop):
            fut_t[128 * j : 128 * j + 128, :] = xbuf[2, :, 128 * j : 128 * j + 128].T

    step = blocks // 4
    series[0].wait()
    stage(jnp.int32(0))
    count(0, step)
    series[1].wait()
    count(step, blocks)
    met()
    p0(0)
    for s in (1, 2):
        first = s * blocks
        if s == 1:
            series[2].wait()
        count(first, first + step)
        if s == 2:
            q4(0)
            p4(0)
        q1(s - 1)
        p1(s - 1)
        count(first + step, first + 2 * step)
        if s == 2:
            q5(0)
        q2(s - 1)
        p2(s - 1)
        count(first + 2 * step, first + 3 * step)
        if s == 2:
            q6(0)
        q3(s - 1)
        p3(s - 1)
        count(first + 3 * step, first + blocks)
        p0(s)
    turn(0, 2)
    q1(2)
    p1(2)
    q4(1)
    p4(1)
    turn(2, 4)
    q2(2)
    p2(2)
    q5(1)
    turn(4, 6)
    q3(2)
    p3(2)
    q6(1)
    turn(6, blocks)
    q4(2)
    p4(2)
    q5(2)
    q6(2)

    make_table(day_total, tot, zone, region, width, offset, table.at[z, x, k])

    def piece(z_at, x_at):
        return table.at[z_at, x_at, k]

    def spread(j, z_at):
        held["r", j] = run([remote(piece(z_at, x), piece(z_at, x), gs_r.at[j], gr_r.at[j], to_right)])[0]
        held["l", j] = run([remote(piece(z_at, x), piece(z_at, x), gs_l.at[j], gr_l.at[j], to_left)])[0]
        held["k", j] = run([remote(piece(z_at, x), piece(z_at, x), gs_k.at[j], gr_k.at[j], other)])[0]

    zs = run(
        [
            remote(piece(z, x), piece(z, x), gs_z.at[j - 1], gr_z.at[j - 1],
                   tm_of(lax.rem(z + j, NZ), x, k))
            for j in range(1, NZ)
        ]
    )
    spread(0, z)
    back = [lax.rem(z + NZ - j, NZ) for j in range(NZ)]
    passed = lax.rem(x + NX - 1 + 2 * k, NX)
    onward = tm_of(z, lax.rem(x + 1 + 2 * k, NX), k)

    def relay(j):
        held["r", j].wait_recv()
        held["l", j].wait_recv()
        z_at = back[j]
        held["f", j] = run([remote(piece(z_at, passed), piece(z_at, passed), gs_f.at[j], gr_f.at[j], onward)])[0]
        for i, at in enumerate((left, right)):
            n = 4 + 4 * i + j
            held["k", n] = run([remote(piece(z_at, at), piece(z_at, at), gs_k.at[n], gr_k.at[n], other)])[0]

    def finish(j):
        held["f", j].wait_recv()
        z_at = back[j]
        held["k", 12 + j] = run(
            [remote(piece(z_at, across), piece(z_at, across), gs_k.at[12 + j], gr_k.at[12 + j], other)]
        )[0]

    zs[0].wait_recv()
    spread(1, back[1])
    relay(0)
    zs[1].wait_recv()
    spread(2, back[2])
    zs[2].wait_recv()
    spread(3, back[3])
    relay(1)
    finish(0)
    relay(2)
    finish(1)
    relay(3)
    finish(2)
    finish(3)
    for j in range(4 * NZ):
        held["k", j].wait_recv()
    for copy in started:
        copy.wait_send()


def map_table(hist_bin, obs_bin, fut_bin, region, width, offset, day_total):
    days, cells = hist_bin.shape
    vmem = pl.BlockSpec(memory_space=pltpu.VMEM)
    hbm = pl.BlockSpec(memory_space=pltpu.HBM)
    dma = pltpu.SemaphoreType.DMA
    block = (NZ, ROWS, BINS)
    small = (8, 128)
    return pl.pallas_call(
        functools.partial(main_kernel, float(day_total)),
        out_shape=(
            jax.ShapeDtypeStruct((NZ, NX, NK, ROWS, BINS), F32),
            jax.ShapeDtypeStruct((cells, days), jnp.int32),
        ),
        in_specs=[hbm, hbm, hbm, vmem, vmem, vmem],
        out_specs=(vmem, vmem),
        scratch_shapes=[
            pltpu.VMEM((3, days, cells), jnp.int32),
            pltpu.VMEM((2, 3, 128, days), BF16),
            pltpu.VMEM((3, NZ, NX, NK, ROWS, BINS), F32),
            pltpu.VMEM((3, NK, REGIONS, 128), F32),
            pltpu.VMEM((3, 4, *block), F32),
            pltpu.VMEM((3, 4, *block), F32),
            pltpu.VMEM((3, 2, 2, ROWS, BINS), F32),
            pltpu.VMEM((3, 2, *block), F32),
            pltpu.VMEM((3, *block), F32),
            pltpu.VMEM((3, 3, ROWS, BINS), F32),
            pltpu.VMEM((3, ROWS, BINS), F32),
            pltpu.VMEM((3, NK, NX, NZ, *small), F32),
            pltpu.VMEM((3, REGIONS, 128), F32),
            pltpu.VMEM((3, NZ, NX, *small), F32),
            pltpu.VMEM((3, 3, NZ, *small), F32),
            pltpu.VMEM((3, NZ, *small), F32),
            pltpu.VMEM((3, 3, NZ, *small), F32),
            pltpu.VMEM((3, NZ, *small), F32),
            pltpu.VMEM((3, 7, NZ, *small), F32),
            dma((3,)),
            dma((3, 4)), dma((3, 4)), dma((3, 2)), dma((3, 2)), dma((3, 4)), dma((3, 4)), dma((3, 3)), dma((3, 3)),
            dma((3,)), dma((3,)), dma((3, 3)), dma((3, 3)), dma((3, 3)), dma((3, 3)), dma((3, 7)), dma((3, 7)),
            dma((3, 3)), dma((3, 3)), dma((3,)), dma((3,)),
            dma((3,)), dma((3,)), dma((4,)), dma((4,)), dma((4,)), dma((4,)), dma((4,)), dma((4,)),
            dma((16,)), dma((16,)),
        ],
        compiler_params=pltpu.CompilerParams(
            collective_id=0, has_side_effects=True, vmem_limit_bytes=48 * 2**20
        ),
        name="map_table",
    )(hist_bin, obs_bin, fut_bin, *(a.reshape(-1, 128) for a in (region, width, offset)))


def apply_kernel(x_ref, t_ref, o_ref):
    low = t_ref[:, 0:128]
    high = t_ref[:, 128:256]
    for at in range(0, x_ref.shape[1], 128):
        idx = x_ref[:, at : at + 128]
        inner = idx & 127
        a = jnp.take_along_axis(low, inner, axis=1)
        b = jnp.take_along_axis(high, inner, axis=1)
        o_ref[at : at + 128, :] = jnp.where(idx >= 128, b, a).T


def apply_table(fut_t, table):
    cells, days = fut_t.shape
    return pl.pallas_call(
        apply_kernel,
        grid=(cells // 128,),
        in_specs=[
            pl.BlockSpec((128, days), lambda j: (j, 0)),
            pl.BlockSpec((128, BINS), lambda j: (j, 0)),
        ],
        out_specs=pl.BlockSpec((days, 128), lambda j: (0, j)),
        out_shape=jax.ShapeDtypeStruct((days, cells), F32),
        name="apply",
    )(fut_t, table)


def body(hist_bin, obs_bin, fut_bin, region_id, bin_width, bin_offset):
    days = hist_bin.shape[0] * lax.axis_size("tm")
    table, fut_t = map_table(hist_bin, obs_bin, fut_bin, region_id, bin_width, bin_offset, days)
    return apply_table(fut_t, table.reshape(-1, BINS))


def solution(mesh):
    placed = (
        P("tm", "cells"),
        P("tm", "cells"),
        P("tm", "cells"),
        P("cells"),
        P("cells"),
        P("cells"),
    )
    return jax.shard_map(
        body, mesh=mesh, in_specs=placed, out_specs=P("tm", "cells"), check_vma=False
    )
```

time: 1000 us -> 95.9 us (0.10)
  other arithmetic: 606 us -> 0 us
  waiting for transfers between devices: 280 us -> 0 us
  Pallas kernels: 0 us -> 89.5 us
  local copies, waits for them, and re-layouts: 80.2 us -> 6 us
  between operations: 14.9 us -> 0.02 us
    reduce_sum x66 -> x0, other arithmetic: 473 us -> none  [the longest x32 297 us: add_block(): return totals + jnp.sum(matches, axis=1, dtype=jnp.float32)]
    psum x1 -> x0, waiting for transfers between devices: 253 us -> none  [body(): zone_counts = lax.psum(zone_part, ('tm', 'cells'))]
    add x34 -> x0, other arithmetic: 126 us -> none  [the longest x32 126 us: add_block(): return totals + jnp.sum(matches, axis=1, dtype=jnp.float32)]
    pallas_call x0 -> x2, Pallas kernels: none -> 89.5 us  [the longest x1 81.9 us: map_table(): pl.pallas_call(functools.partial(main_kernel, float(day_total)), out_shap...]
    dynamic_slice x34 -> x0, local copies, waits for them, and re-layouts: 31.6 us -> none  [the longest x32 30.1 us: add_block(): lax.dynamic_slice_in_dim(stacked, turn_index * day_block, day_block, 1)]
    eq x32 -> x0, local copies, waits for them, and re-layouts: 27 us -> none  [select_rows(): matches = bins_rows[..., None] == levels]
    all_to_all x1 -> x0, waiting for transfers between devices: 26.6 us -> none  [copy_for_each(): lax.all_to_all(jnp.broadcast_to(array[None], (count, *array.shape)), axis...]
    dynamic_update_slice x32 -> x0, local copies, waits for them, and re-layouts: 20.5 us -> none  [apply_table(): return lax.map(select_rows, folded).reshape(day_count, cell_count)]
  transfers between devices with their start and end apart: 3 -> 0, of which waited for: 2 -> 0; matrix products, arithmetic and copies ran while one was open for 0% -> 0% of each run, Pallas kernels for 0% -> 0%
where the time goes in v2:
time: 95.9 us; the launch traced here: 95.6 us
  Pallas kernels  89.5 us (93%)
  local copies, waits for them, and re-layouts  6 us (6%)
    pallas_call x1, Pallas kernels, map_table(): pl.pallas_call(functools.partial(main_kernel, float(day_total)), out_shap...  81.9 us
    pallas_call x1, Pallas kernels, apply_table(): pl.pallas_call(apply_kernel, grid=(cells // 128,), in_specs=[pl.BlockSpec...  7.6 us
    unnamed x12, local copies, waits for them, and re-layouts  6 us

profile of v2, /device:TPU:1, one launch (start us, length us, event | category | flops | bytes accessed | tf_op | source)
XLA Modules:
  0.0 95.6 jit_solution(2893231660222553381)
XLA Ops:
  0.0 0.0 copy-start
  0.0 1.6 %copy-done = s32[512,1024]{1,0:T(8,128)S(1)} copy-done((s32[512,1024]{1,0:T(8,128)S(1)}, s32[512,1024]{1,0:T(8,128)}, u32[]{:S(2)}) %copy-start) | copy-done | bytes 2097176
  1.6 0.0 copy-start.3
  1.6 0.7 copy-done.3
  2.3 0.0 copy-start.4
  2.3 0.7 copy-done.4
  3.0 0.0 copy-start.5
  3.0 0.7 copy-done.5
  3.7 81.9 %map_table.1 = (f32[4,4,2,32,256]{4,3,2,1,0:T(8,128)S(1)}, s32[1024,512]{1,0:T(8,128)S(1)}) custom-call(s32[512,1024]{1,0:T(8,128)S(1)} %copy-done, s32[512,1024]{1,0:T(8,128)} %obs.1, s32[512,1024]{1,0:T(8,128)} %fut.1, s32[8,128]{1,0:T(8,128)S(1)} %bitcast.5, f32[8,128]{1,0:T(8,128)S(1)} %bitcast.6, f32[8,128]{1,0:T(8,128)S(1)} %bitcast.7), custom_call_target="tpu_custom_call" | custom-call | tf_op jit(solution)/shard_map/map_table/pallas_call | solution.py:466
  85.6 0.0 copy-start.1
  85.6 1.3 %copy-done.1 = s32[1024,512]{1,0:T(8,128)} copy-done((s32[1024,512]{1,0:T(8,128)}, s32[1024,512]{1,0:T(8,128)S(1)}, u32[]{:S(2)}) %copy-start.1) | copy-done | bytes 2097176
  87.0 0.0 copy-start.2
  87.0 1.0 %copy-done.2 = f32[4,4,2,32,256]{4,3,2,1,0:T(8,128)} copy-done((f32[4,4,2,32,256]{4,3,2,1,0:T(8,128)}, f32[4,4,2,32,256]{4,3,2,1,0:T(8,128)S(1)}, u32[]{:S(2)}) %copy-start.2) | copy-done | bytes 1048600
  88.0 7.6 %apply.1 = f32[512,1024]{1,0:T(8,128)} custom-call(s32[1024,512]{1,0:T(8,128)} %copy-done.1, f32[1024,256]{1,0:T(8,128)} %bitcast.4), custom_call_target="tpu_custom_call" | custom-call | tf_op jit(solution)/shard_map/apply/pallas_call | solution.py:521
Async XLA Ops:
  0.0 1.6 %copy-start = (s32[512,1024]{1,0:T(8,128)S(1)}, s32[512,1024]{1,0:T(8,128)}, u32[]{:S(2)}) copy-start(s32[512,1024]{1,0:T(8,128)} %hist.1) | copy-start | bytes 6291460
  1.6 0.7 copy-start.3
  2.3 0.7 copy-start.4
  3.0 0.7 copy-start.5
  85.6 1.4 %copy-start.1 = (s32[1024,512]{1,0:T(8,128)}, s32[1024,512]{1,0:T(8,128)S(1)}, u32[]{:S(2)}) copy-start(s32[1024,512]{1,0:T(8,128)S(1)} %get-tuple-element.7.x_ref) | copy-start | bytes 6291460
  87.0 1.0 %copy-start.2 = (f32[4,4,2,32,256]{4,3,2,1,0:T(8,128)}, f32[4,4,2,32,256]{4,3,2,1,0:T(8,128)S(1)}, u32[]{:S(2)}) copy-start(f32[4,4,2,32,256]{4,3,2,1,0:T(8,128)S(1)} %get-tuple-element.8) | copy-start | bytes 3145732

commit v3 on v2

--- a/solution.py
+++ b/solution.py
@@ -11,6 +11,7 @@
 REGIONS = 128
 F32 = jnp.float32
 BF16 = jnp.bfloat16
+F8 = jnp.float8_e4m3fn
 POOL_WEIGHT = 0.5
 
 NZ, NX, NK = 4, 4, 2
@@ -20,10 +21,8 @@
 
 def stage_block(bins, planes, slot):
     xt = bins.T
-    hi = xt >> 4
     planes[slot, 0] = (xt & 15).astype(BF16)
-    planes[slot, 1] = (hi & 7).astype(BF16)
-    planes[slot, 2] = jnp.where(hi >= 8, 1024.0, 1.0).astype(BF16)
+    planes[slot, 1] = (xt >> 4).astype(BF16)
 
 
 def count_block(planes, slot):
@@ -31,24 +30,33 @@
     one = jnp.ones((), BF16)
     row = lax.broadcasted_iota(jnp.int32, (8, 128), 0)
     lane = lax.broadcasted_iota(jnp.int32, (8, 128), 1)
-    column = lane // 8
+    second = (lane % 16) >= 8
+    slot_of = lane // 16
+    idx = (lane % 8) * 16 + ((lane // 8) % 2) * 8 + row
     low, high = [], []
     for q in range(8):
         rows = slice(16 * q, 16 * q + 16)
-        lo, hi, weight = planes[slot, 0, rows], planes[slot, 1, rows], planes[slot, 2, rows]
-        lhs = jnp.concatenate([jnp.where(hi == float(h), weight, zero) for h in range(8)], 0)
+        lo, hi = planes[slot, 0, rows], planes[slot, 1, rows]
+        lhs = jnp.concatenate([jnp.where(hi == float(h), one, zero) for h in range(16)], 0)
         rhs = jnp.concatenate([jnp.where(lo == float(l), one, zero) for l in range(16)], 0)
-        out = lax.dot_general(lhs, rhs, (((1,), (1,)), ((), ())), preferred_element_type=F32)
-        for half in range(2):
-            idx = (lane % 8) * 16 + half * 8 + row
-            packed = jnp.zeros((8, 128), F32)
+        out = lax.dot_general(
+            lhs.astype(F8), rhs.astype(F8), (((1,), (1,)), ((), ())), preferred_element_type=F32
+        )
+        out = out[0:128] + 1024.0 * out[128:256]
+        parts = []
+        for m in range(2):
+            part = None
             for h in range(8):
-                for m in range(2):
-                    at = 16 * h + 8 * half
-                    piece = out[at : at + 8, 128 * m : 128 * m + 128]
-                    packed = jnp.where(
-                        column == 2 * h + m, jnp.take_along_axis(piece, idx, axis=1), packed
-                    )
+                at = 16 * h
+                a = out[at : at + 8, 128 * m : 128 * m + 128]
+                b = out[at + 8 : at + 16, 128 * m : 128 * m + 128]
+                own = jnp.take_along_axis(jnp.where(second, b, a), idx, axis=1)
+                part = own if h == 0 else jnp.where(slot_of == h, own, part)
+            parts.append(part)
+        for packed in (
+            jnp.where(second, pltpu.roll(parts[1], 8, 1), parts[0]),
+            jnp.where(second, parts[1], pltpu.roll(parts[0], 120, 1)),
+        ):
             upper = jnp.floor(packed * (1.0 / 1024.0))
             low.append(packed - 1024.0 * upper)
             high.append(upper)
@@ -92,11 +100,7 @@
     ).astype(F32)
     pooled, stacked = [], []
     for s in range(3):
-        halves = []
-        for k in range(NK):
-            rows = [zone[s, k, x, z] for z in range(NZ) for x in range(NX)]
-            halves.append(jnp.concatenate(rows, 0))
-        mine = exact_dot(pick, jnp.concatenate(halves, 1))
+        mine = exact_dot(pick, jnp.concatenate([zone[s, k].reshape(REGIONS, 128) for k in range(NK)], 1))
         share = mine / jnp.sum(mine, axis=1, keepdims=True)
         pooled.append(tot[s] + POOL_WEIGHT * day_total * share)
     filled = [pooled[s] / jnp.maximum(pooled[s], 1.0) for s in range(2)]
@@ -152,11 +156,11 @@
 
 
 def main_kernel(
-    day_total, hist, obs, fut, region, width, offset, table, fut_t,
+    day_total, hist, obs, fut, reg_in, wid_in, off_in, table, fut_t, reg, wid, off,
     xbuf, planes, cnt, zin, core_in, acc, far_in, side_in, done, last_in, tot,
-    zone, z_core, z_acc, z_x, z_acc2, z_y, z_acc3, z_z,
+    zone, z_core, z_acc, z_x, z_acc2, z_z,
     s_in, s_core, r_core, s_far, r_far, s_side, r_side, s_last, r_last,
-    zs_core, zr_core, zs_x, zr_x, zs_y, zr_y, zs_z, zr_z, zs_gx, zr_gx, zs_gk, zr_gk,
+    zs_core, zr_core, zs_x, zr_x, zs_z, zr_z, zs_gx, zr_gx, zs_gk, zr_gk,
     gs_z, gr_z, gs_r, gr_r, gs_l, gr_l, gs_f, gr_f, gs_k, gr_k,
 ):
     z, x, k = place()
@@ -169,23 +173,30 @@
     to_right, to_left = tm_of(z, right, k), tm_of(z, left, k)
     order = (across, right, left, x)
 
-    series = [
-        pltpu.make_async_copy(ref, xbuf.at[s], s_in.at[s])
-        for s, ref in enumerate((hist, obs, fut))
+    lead = pltpu.make_async_copy(hist.at[:, 0:128], xbuf.at[0, :, 0:128], s_in.at[0])
+    lead.start()
+    small = [
+        pltpu.make_async_copy(ref, to, s_in.at[4 + i])
+        for i, (ref, to) in enumerate(((reg_in, reg), (wid_in, wid), (off_in, off)))
     ]
-    for copy in series:
+    small[0].start()
+    series = [pltpu.make_async_copy(hist.at[:, 128:], xbuf.at[0, :, 128:], s_in.at[1])]
+    series += [
+        pltpu.make_async_copy(ref, xbuf.at[s], s_in.at[1 + s]) for s, ref in ((1, obs), (2, fut))
+    ]
+    for copy in series + small[1:]:
         copy.start()
     y, z_hi = c // 2, lax.rem(c, 2)
     z_full = z_hi * NZ + z
-    along_y = [lax.rem(y + j, 4) * 2 + z_hi for j in range(1, 4)]
+    plane = x * 4 + y
+    across_plane = [lax.rem(plane + j, 16) for j in range(1, 16)]
+    in_plane = [(tm_of(z, at // 4, k), lax.rem(at, 4) * 2 + z_hi) for at in across_plane]
     along_z = []
     for j in range(1, 2 * NZ):
         at = lax.rem(z_full + j, 2 * NZ)
         along_z.append((tm_of(lax.rem(at, NZ), x, k), y * 2 + at // NZ))
     partners = [{"tm": other}]
-    partners += [{"tm": tm_of(z, lax.rem(x + j, NX), k)} for j in range(1, NX)]
-    partners += [{"cells": at} for at in along_y]
-    partners += [{"tm": a, "cells": b} for a, b in along_z]
+    partners += [{"tm": a, "cells": b} for a, b in in_plane + along_z]
     met = greet(partners)
     zin[...] = jnp.zeros_like(zin)
 
@@ -203,16 +214,24 @@
             s = n // blocks
             j = lax.rem(n, blocks)
             zones = lax.broadcasted_iota(jnp.int32, (REGIONS, 128), 0)
-            pick = (zones == region[pl.ds(j, 1), :]).astype(BF16)
-            for half, part in enumerate(count_block(planes, lax.rem(n, 2))):
+            pick = (zones == reg[pl.ds(j, 1), :]).astype(BF16)
+            counts = count_block(planes, lax.rem(n, 2))
+            heads, rests = [], []
+            for half, part in enumerate(counts):
                 cnt[s, j // 2, pl.ds(lax.rem(j, 2) * 2, 2), :, :, 128 * half : 128 * half + 128] = (
                     part.reshape(2, NK, ROWS, 128)
                 )
                 head = jnp.minimum(part, 256.0)
-                rest = part - head
-                zin[s, half] += jnp.dot(
-                    pick, head.astype(BF16), preferred_element_type=F32
-                ) + jnp.dot(pick, rest.astype(BF16), preferred_element_type=F32)
+                heads.append(head.astype(BF16))
+                rests.append((part - head).astype(BF16))
+            both = jnp.concatenate(
+                [jnp.concatenate(heads, 1), jnp.concatenate(rests, 1)], 0
+            )
+            sums = jnp.dot(
+                jnp.concatenate([pick, pick], 1), both, preferred_element_type=F32
+            )
+            zin[s, 0] += sums[:, 0:128]
+            zin[s, 1] += sums[:, 128:256]
             return carry
 
         lax.fori_loop(first, stop, one, 0)
@@ -291,33 +310,26 @@
 
     def q1(s):
         held["zc", s][0].wait_recv()
-        z_acc[s] = zin[s, k].reshape(NZ, NX, 8, 128) + z_core[s].reshape(NZ, NX, 8, 128)
+        z_acc[s] = (zin[s, k] + z_core[s]).reshape(16, 8, 128)
         held["zx", s] = run(
             [
-                remote(z_acc.at[s, :, lax.rem(x + j, NX)], z_x.at[s, j - 1], zs_x.at[s, j - 1],
-                       zr_x.at[s, j - 1], tm_of(z, lax.rem(x + j, NX), k))
-                for j in range(1, NX)
+                remote(z_acc.at[s, at], z_x.at[s, j], zs_x.at[s, j], zr_x.at[s, j], *in_plane[j])
+                for j, at in enumerate(across_plane)
             ]
         )
 
     def q2(s):
         for copy in held["zx", s]:
             copy.wait_recv()
-        z_acc2[s] = z_acc[s, :, x] + z_x[s, 0] + z_x[s, 1] + z_x[s, 2]
-        held["zy", s] = run(
-            [
-                remote(z_acc2.at[s], z_y.at[s, j], zs_y.at[s, j], zr_y.at[s, j], tm, at)
-                for j, at in enumerate(along_y)
-            ]
-        )
+        total = z_acc[s, plane]
+        for j in range(15):
+            total = total + z_x[s, j]
+        z_acc2[s] = total
 
     def q3(s):
-        for copy in held["zy", s]:
-            copy.wait_recv()
-        z_acc3[s] = z_acc2[s] + z_y[s, 0] + z_y[s, 1] + z_y[s, 2]
         held["zz", s] = run(
             [
-                remote(z_acc3.at[s], z_z.at[s, j], zs_z.at[s, j], zr_z.at[s, j], *at)
+                remote(z_acc2.at[s], z_z.at[s, j], zs_z.at[s, j], zr_z.at[s, j], *at)
                 for j, at in enumerate(along_z)
             ]
         )
@@ -325,19 +337,20 @@
     def q4(s):
         for copy in held["zz", s]:
             copy.wait_recv()
-        total = z_acc3[s]
+        total = z_acc2[s]
         for j in range(2 * NZ - 1):
             total = total + z_z[s, j]
-        zone[s, k, x] = total
+        zone[s, k, plane] = total
+
+    def q5(s):
         held["gx", s] = run(
             [
-                remote(zone.at[s, k, x], zone.at[s, k, x], zs_gx.at[s, j - 1], zr_gx.at[s, j - 1],
-                       tm_of(z, lax.rem(x + j, NX), k))
-                for j in range(1, NX)
-            ]
-        )
-
-    def q5(s):
+                remote(zone.at[s, k, plane], zone.at[s, k, plane], zs_gx.at[s, j], zr_gx.at[s, j], *at)
+                for j, at in enumerate(in_plane)
+            ]
+        )
+
+    def q55(s):
         for copy in held["gx", s]:
             copy.wait_recv()
         held["gk", s] = run([remote(zone.at[s, k], zone.at[s, k], zs_gk.at[s], zr_gk.at[s], other)])
@@ -350,8 +363,10 @@
             fut_t[128 * j : 128 * j + 128, :] = xbuf[2, :, 128 * j : 128 * j + 128].T
 
     step = blocks // 4
+    lead.wait()
+    stage(jnp.int32(0))
+    small[0].wait()
     series[0].wait()
-    stage(jnp.int32(0))
     count(0, step)
     series[1].wait()
     count(step, blocks)
@@ -363,42 +378,43 @@
             series[2].wait()
         count(first, first + step)
         if s == 2:
-            q4(0)
             p4(0)
         q1(s - 1)
         p1(s - 1)
         count(first + step, first + 2 * step)
         if s == 2:
-            q5(0)
+            q55(0)
         q2(s - 1)
+        q3(s - 1)
         p2(s - 1)
         count(first + 2 * step, first + 3 * step)
         if s == 2:
             q6(0)
-        q3(s - 1)
         p3(s - 1)
         count(first + 3 * step, first + blocks)
         p0(s)
-    turn(0, 2)
+        q4(s - 1)
+        q5(s - 1)
     q1(2)
     p1(2)
-    q4(1)
     p4(1)
-    turn(2, 4)
+    turn(0, 4)
     q2(2)
+    q3(2)
     p2(2)
-    q5(1)
-    turn(4, 6)
-    q3(2)
+    q55(1)
+    turn(4, blocks)
     p3(2)
+    q4(2)
+    q5(2)
+    p4(2)
     q6(1)
-    turn(6, blocks)
-    q4(2)
-    p4(2)
-    q5(2)
+    small[1].wait()
+    small[2].wait()
+    q55(2)
     q6(2)
 
-    make_table(day_total, tot, zone, region, width, offset, table.at[z, x, k])
+    make_table(day_total, tot, zone, reg, wid, off, table.at[z, x, k])
 
     def piece(z_at, x_at):
         return table.at[z_at, x_at, k]
@@ -469,11 +485,14 @@
             jax.ShapeDtypeStruct((NZ, NX, NK, ROWS, BINS), F32),
             jax.ShapeDtypeStruct((cells, days), jnp.int32),
         ),
-        in_specs=[hbm, hbm, hbm, vmem, vmem, vmem],
+        in_specs=[hbm] * 6,
         out_specs=(vmem, vmem),
         scratch_shapes=[
+            pltpu.VMEM((8, 128), jnp.int32),
+            pltpu.VMEM((8, 128), F32),
+            pltpu.VMEM((8, 128), F32),
             pltpu.VMEM((3, days, cells), jnp.int32),
-            pltpu.VMEM((2, 3, 128, days), BF16),
+            pltpu.VMEM((2, 2, 128, days), BF16),
             pltpu.VMEM((3, NZ, NX, NK, ROWS, BINS), F32),
             pltpu.VMEM((3, NK, REGIONS, 128), F32),
             pltpu.VMEM((3, 4, *block), F32),
@@ -483,33 +502,35 @@
             pltpu.VMEM((3, *block), F32),
             pltpu.VMEM((3, 3, ROWS, BINS), F32),
             pltpu.VMEM((3, ROWS, BINS), F32),
-            pltpu.VMEM((3, NK, NX, NZ, *small), F32),
+            pltpu.VMEM((3, NK, 16, *small), F32),
             pltpu.VMEM((3, REGIONS, 128), F32),
-            pltpu.VMEM((3, NZ, NX, *small), F32),
-            pltpu.VMEM((3, 3, NZ, *small), F32),
-            pltpu.VMEM((3, NZ, *small), F32),
-            pltpu.VMEM((3, 3, NZ, *small), F32),
-            pltpu.VMEM((3, NZ, *small), F32),
-            pltpu.VMEM((3, 7, NZ, *small), F32),
-            dma((3,)),
+            pltpu.VMEM((3, 16, *small), F32),
+            pltpu.VMEM((3, 15, *small), F32),
+            pltpu.VMEM((3, *small), F32),
+            pltpu.VMEM((3, 7, *small), F32),
+            dma((7,)),
             dma((3, 4)), dma((3, 4)), dma((3, 2)), dma((3, 2)), dma((3, 4)), dma((3, 4)), dma((3, 3)), dma((3, 3)),
-            dma((3,)), dma((3,)), dma((3, 3)), dma((3, 3)), dma((3, 3)), dma((3, 3)), dma((3, 7)), dma((3, 7)),
-            dma((3, 3)), dma((3, 3)), dma((3,)), dma((3,)),
+            dma((3,)), dma((3,)), dma((3, 15)), dma((3, 15)), dma((3, 7)), dma((3, 7)),
+            dma((3, 15)), dma((3, 15)), dma((3,)), dma((3,)),
             dma((3,)), dma((3,)), dma((4,)), dma((4,)), dma((4,)), dma((4,)), dma((4,)), dma((4,)),
             dma((16,)), dma((16,)),
         ],
         compiler_params=pltpu.CompilerParams(
-            collective_id=0, has_side_effects=True, vmem_limit_bytes=48 * 2**20
+            collective_id=0, has_side_effects=True, vmem_limit_bytes=58 * 2**20
         ),
         name="map_table",
     )(hist_bin, obs_bin, fut_bin, *(a.reshape(-1, 128) for a in (region, width, offset)))
 
 
+APPLY = 256
+
+
 def apply_kernel(x_ref, t_ref, o_ref):
-    low = t_ref[:, 0:128]
-    high = t_ref[:, 128:256]
+    rows = pl.ds(pl.multiple_of(pl.program_id(0) * APPLY, APPLY), APPLY)
+    low = t_ref[rows, 0:128]
+    high = t_ref[rows, 128:256]
     for at in range(0, x_ref.shape[1], 128):
-        idx = x_ref[:, at : at + 128]
+        idx = x_ref[rows, at : at + 128]
         inner = idx & 127
         a = jnp.take_along_axis(low, inner, axis=1)
         b = jnp.take_along_axis(high, inner, axis=1)
@@ -518,14 +539,12 @@
 
 def apply_table(fut_t, table):
     cells, days = fut_t.shape
+    vmem = pl.BlockSpec(memory_space=pltpu.VMEM)
     return pl.pallas_call(
         apply_kernel,
-        grid=(cells // 128,),
-        in_specs=[
-            pl.BlockSpec((128, days), lambda j: (j, 0)),
-            pl.BlockSpec((128, BINS), lambda j: (j, 0)),
-        ],
-        out_specs=pl.BlockSpec((days, 128), lambda j: (0, j)),
+        grid=(cells // APPLY,),
+        in_specs=[vmem, vmem],
+        out_specs=pl.BlockSpec((days, APPLY), lambda j: (0, j)),
         out_shape=jax.ShapeDtypeStruct((days, cells), F32),
         name="apply",
     )(fut_t, table)

time: 95.9 us -> 87.4 us (0.911)
  local copies, waits for them, and re-layouts: 6 us -> 0 us
  Pallas kernels: 89.5 us -> 87.3 us
    unnamed x12 -> x0, local copies, waits for them, and re-layouts: 6 us -> none
    pallas_call x1, Pallas kernels: 7.6 us -> 6.44 us  [apply_table(): pl.pallas_call(apply_kernel, grid=(cells // APPLY,), in_specs=[vmem, vmem...]
    pallas_call x1, Pallas kernels: 81.9 us -> 80.8 us  [map_table(): pl.pallas_call(functools.partial(main_kernel, float(day_total)), out_shap...]
where the time goes in v3:
time: 87.4 us; the launch traced here: 87.3 us
  Pallas kernels  87.3 us (100%)
    pallas_call x1, Pallas kernels, map_table(): pl.pallas_call(functools.partial(main_kernel, float(day_total)), out_shap...  80.8 us
    pallas_call x1, Pallas kernels, apply_table(): pl.pallas_call(apply_kernel, grid=(cells // APPLY,), in_specs=[vmem, vmem...  6.44 us

profile of v3, /device:TPU:1, one launch (start us, length us, event | category | flops | bytes accessed | tf_op | source)
XLA Modules:
  0.0 87.3 jit_solution(17645532039674727604)
XLA Ops:
  0.0 80.8 %map_table.1 = (f32[4,4,2,32,256]{4,3,2,1,0:T(8,128)}, s32[1024,512]{1,0:T(8,128)}) custom-call(s32[512,1024]{1,0:T(8,128)} %hist.1, s32[512,1024]{1,0:T(8,128)} %obs.1, s32[512,1024]{1,0:T(8,128)} %fut.1, s32[8,128]{1,0:T(8,128)} %bitcast.5, f32[8,128]{1,0:T(8,128)} %bitcast.6, f32[8,128]{1,0:T(8,128)} %bitcast.7), custom_call_target="tpu_custom_call" | custom-call | tf_op jit(solution)/shard_map/map_table/pallas_call | solution.py:482
  80.8 6.4 %apply.1 = f32[512,1024]{1,0:T(8,128)} custom-call(s32[1024,512]{1,0:T(8,128)} %get-tuple-element.7.x_ref, f32[1024,256]{1,0:T(8,128)} %bitcast.4), custom_call_target="tpu_custom_call" | custom-call | tf_op jit(solution)/shard_map/apply/pallas_call | solution.py:543

commit v4 on v3

--- a/solution.py
+++ b/solution.py
@@ -21,13 +21,18 @@
 
 def stage_block(bins, planes, slot):
     xt = bins.T
-    planes[slot, 0] = (xt & 15).astype(BF16)
-    planes[slot, 1] = (xt >> 4).astype(BF16)
+    less = (lax.broadcasted_iota(jnp.int32, (32, bins.shape[0]), 0) >= 16).astype(jnp.int32)
+    for q in range(8):
+        rows = xt[16 * q : 16 * q + 16]
+        twice = jnp.concatenate([rows, rows], 0)
+        planes[slot, 0, q] = ((twice & 15) - less).astype(jnp.int8)
+        planes[slot, 1, q] = ((twice >> 4) - less).astype(jnp.int8)
 
 
 def count_block(planes, slot):
-    zero = jnp.zeros((), BF16)
-    one = jnp.ones((), BF16)
+    zero = jnp.zeros((), F8)
+    one = jnp.ones((), F8)
+    digits = [jnp.int8(d) for d in range(0, 16, 2)]
     row = lax.broadcasted_iota(jnp.int32, (8, 128), 0)
     lane = lax.broadcasted_iota(jnp.int32, (8, 128), 1)
     second = (lane % 16) >= 8
@@ -35,13 +40,10 @@
     idx = (lane % 8) * 16 + ((lane // 8) % 2) * 8 + row
     low, high = [], []
     for q in range(8):
-        rows = slice(16 * q, 16 * q + 16)
-        lo, hi = planes[slot, 0, rows], planes[slot, 1, rows]
-        lhs = jnp.concatenate([jnp.where(hi == float(h), one, zero) for h in range(16)], 0)
-        rhs = jnp.concatenate([jnp.where(lo == float(l), one, zero) for l in range(16)], 0)
-        out = lax.dot_general(
-            lhs.astype(F8), rhs.astype(F8), (((1,), (1,)), ((), ())), preferred_element_type=F32
-        )
+        lo, hi = planes[slot, 0, q], planes[slot, 1, q]
+        lhs = jnp.concatenate([jnp.where(hi == d, one, zero) for d in digits], 0)
+        rhs = jnp.concatenate([jnp.where(lo == d, one, zero) for d in digits], 0)
+        out = lax.dot_general(lhs, rhs, (((1,), (1,)), ((), ())), preferred_element_type=F32)
         out = out[0:128] + 1024.0 * out[128:256]
         parts = []
         for m in range(2):
@@ -492,7 +494,7 @@
             pltpu.VMEM((8, 128), F32),
             pltpu.VMEM((8, 128), F32),
             pltpu.VMEM((3, days, cells), jnp.int32),
-            pltpu.VMEM((2, 2, 128, days), BF16),
+            pltpu.VMEM((2, 2, 8, 32, days), jnp.int8),
             pltpu.VMEM((3, NZ, NX, NK, ROWS, BINS), F32),
             pltpu.VMEM((3, NK, REGIONS, 128), F32),
             pltpu.VMEM((3, 4, *block), F32),

time: 87.4 us -> 84 us (0.961)
  Pallas kernels: 87.3 us -> 83.9 us
    pallas_call x1, Pallas kernels: 80.8 us -> 77.5 us  [map_table(): pl.pallas_call(functools.partial(main_kernel, float(day_total)), out_shap...]
where the time goes in v4:
time: 84 us; the launch traced here: 83.9 us
  Pallas kernels  83.9 us (100%)
    pallas_call x1, Pallas kernels, map_table(): pl.pallas_call(functools.partial(main_kernel, float(day_total)), out_shap...  77.5 us
    pallas_call x1, Pallas kernels, apply_table(): pl.pallas_call(apply_kernel, grid=(cells // APPLY,), in_specs=[vmem, vmem...  6.44 us

profile of v4, /device:TPU:1, one launch (start us, length us, event | category | flops | bytes accessed | tf_op | source)
XLA Modules:
  0.0 83.9 jit_solution(17459765147583428712)
XLA Ops:
  0.0 77.5 %map_table.1 = (f32[4,4,2,32,256]{4,3,2,1,0:T(8,128)}, s32[1024,512]{1,0:T(8,128)}) custom-call(s32[512,1024]{1,0:T(8,128)} %hist.1, s32[512,1024]{1,0:T(8,128)} %obs.1, s32[512,1024]{1,0:T(8,128)} %fut.1, s32[8,128]{1,0:T(8,128)} %bitcast.5, f32[8,128]{1,0:T(8,128)} %bitcast.6, f32[8,128]{1,0:T(8,128)} %bitcast.7), custom_call_target="tpu_custom_call" | custom-call | tf_op jit(solution)/shard_map/map_table/pallas_call | solution.py:484
  77.5 6.4 %apply.1 = f32[512,1024]{1,0:T(8,128)} custom-call(s32[1024,512]{1,0:T(8,128)} %get-tuple-element.7.x_ref, f32[1024,256]{1,0:T(8,128)} %bitcast.4), custom_call_target="tpu_custom_call" | custom-call | tf_op jit(solution)/shard_map/apply/pallas_call | solution.py:545

commit v5 on v4

--- a/solution.py
+++ b/solution.py
@@ -364,55 +364,58 @@
         for j in range(first, stop):
             fut_t[128 * j : 128 * j + 128, :] = xbuf[2, :, 128 * j : 128 * j + 128].T
 
-    step = blocks // 4
+    half = blocks // 2
     lead.wait()
     stage(jnp.int32(0))
     small[0].wait()
     series[0].wait()
-    count(0, step)
+    count(0, half)
     series[1].wait()
-    count(step, blocks)
+    count(half, 2 * half)
     met()
     p0(0)
-    for s in (1, 2):
-        first = s * blocks
-        if s == 1:
-            series[2].wait()
-        count(first, first + step)
-        if s == 2:
-            p4(0)
-        q1(s - 1)
-        p1(s - 1)
-        count(first + step, first + 2 * step)
-        if s == 2:
-            q55(0)
-        q2(s - 1)
-        q3(s - 1)
-        p2(s - 1)
-        count(first + 2 * step, first + 3 * step)
-        if s == 2:
-            q6(0)
-        p3(s - 1)
-        count(first + 3 * step, first + blocks)
-        p0(s)
-        q4(s - 1)
-        q5(s - 1)
+    count(2 * half, 3 * half)
+    q1(0)
+    p1(0)
+    series[2].wait()
+    count(3 * half, 4 * half)
+    p0(1)
+    q2(0)
+    q3(0)
+    p2(0)
+    count(4 * half, 5 * half)
+    q1(1)
+    p1(1)
+    q4(0)
+    q5(0)
+    p3(0)
+    count(5 * half, 6 * half)
+    p0(2)
+    q2(1)
+    q3(1)
+    p2(1)
     q1(2)
     p1(2)
-    p4(1)
-    turn(0, 4)
+    q55(0)
+    p4(0)
+    turn(0, half)
     q2(2)
     q3(2)
     p2(2)
-    q55(1)
-    turn(4, blocks)
+    p3(1)
+    q4(1)
+    q5(1)
+    q6(0)
+    turn(half, blocks)
     p3(2)
     q4(2)
     q5(2)
+    q55(1)
+    p4(1)
     p4(2)
-    q6(1)
     small[1].wait()
     small[2].wait()
+    q6(1)
     q55(2)
     q6(2)
 

time: 84 us -> 76.6 us (0.912)
  Pallas kernels: 83.9 us -> 76.5 us
    pallas_call x1, Pallas kernels: 77.5 us -> 70.1 us  [map_table(): pl.pallas_call(functools.partial(main_kernel, float(day_total)), out_shap...]
where the time goes in v5:
time: 76.6 us; the launch traced here: 76.5 us
  Pallas kernels  76.5 us (100%)
    pallas_call x1, Pallas kernels, map_table(): pl.pallas_call(functools.partial(main_kernel, float(day_total)), out_shap...  70.1 us
    pallas_call x1, Pallas kernels, apply_table(): pl.pallas_call(apply_kernel, grid=(cells // APPLY,), in_specs=[vmem, vmem...  6.44 us

profile of v5, /device:TPU:1, one launch (start us, length us, event | category | flops | bytes accessed | tf_op | source)
XLA Modules:
  0.0 76.5 jit_solution(5746380269026559148)
XLA Ops:
  0.0 70.1 %map_table.1 = (f32[4,4,2,32,256]{4,3,2,1,0:T(8,128)}, s32[1024,512]{1,0:T(8,128)}) custom-call(s32[512,1024]{1,0:T(8,128)} %hist.1, s32[512,1024]{1,0:T(8,128)} %obs.1, s32[512,1024]{1,0:T(8,128)} %fut.1, s32[8,128]{1,0:T(8,128)} %bitcast.5, f32[8,128]{1,0:T(8,128)} %bitcast.6, f32[8,128]{1,0:T(8,128)} %bitcast.7), custom_call_target="tpu_custom_call" | custom-call | tf_op jit(solution)/shard_map/map_table/pallas_call | solution.py:487
  70.1 6.4 %apply.1 = f32[512,1024]{1,0:T(8,128)} custom-call(s32[1024,512]{1,0:T(8,128)} %get-tuple-element.7.x_ref, f32[1024,256]{1,0:T(8,128)} %bitcast.4), custom_call_target="tpu_custom_call" | custom-call | tf_op jit(solution)/shard_map/apply/pallas_call | solution.py:548
